TPU v7x, 32 devices: a whole 2x2x4 slice. The times are simulated.
32 devices in a mesh: pb: 8 (over y, x, core), ka: 4 (over z).
Axes of the slice: x: 2, y: 2, z: 4, core: 2. Of those that a mesh axis runs over, the one named last changes fastest.
Arguments:
- coupling: bfloat16 [2, 320, 4800, 320], P(None, 'ka', 'pb'), may hold values from -0.019897461 to 0.019897461
- kpoints: int32 [3, 16], replicated, may hold values from 0 to 99
- qpoints: int32 [3, 32], replicated, may hold values from 0 to 99
- electron_cells: int32 [3, 320], replicated, may hold values from -6 to 6
- phonon_cells: int32 [3, 320], replicated, may hold values from -6 to 6
- phonon_modes: bfloat16 [32, 2, 120, 120], P('pb'), may hold values from -0.375 to 0.375
- band_vectors: bfloat16 [32, 16, 2, 40, 40], P('pb', 'ka'), may hold values from -0.625 to 0.625
- energies_kq: float32 [32, 16, 40], P('pb', 'ka'), may hold values from -0.5 to 0.5
- occupations_kq: float32 [32, 16, 40], P('pb', 'ka'), may hold values from 0 to 1
- energy_k: float32 [16], P('ka'), may hold values from -0.5 to 0.5
- occupation_k: float32 [16], P('ka'), may hold values from 0 to 1
- frequencies: float32 [32, 120], P('pb'), may hold values from 0.02 to 0.2
- bose_factors: float32 [32, 120], P('pb'), may hold values from 0.1 to 5
Outputs:
- electron_width: float32 [16, 120], P('ka')
- phonon_width: float32 [32, 120], P('pb')
All inputs are finite; a program needn't handle non-finite values.
Results may differ from a plain program's by a relative error of at most 0.0066.
Values may be sent and summed in bfloat16 or wider, within the bound.
A program may use at most 320 MiB of HBM per device.

v0:
```python
import functools
import math

import jax
import jax.numpy as jnp
from jax import lax
from jax.experimental import pallas as pl
from jax.experimental.pallas import tpu as pltpu
from jax.sharding import PartitionSpec as P

NB = 40
MODES = 120
NG = 100


smearing = 0.05


def phase_table(points, cells):
    product = (
        points[0][:, None] * cells[0][None, :]
        + points[1][:, None] * cells[1][None, :]
        + points[2][:, None] * cells[2][None, :]
    )
    angle = jnp.mod(product, NG).astype(jnp.float32) * (2.0 * math.pi / NG)
    return (jnp.cos(angle).astype(jnp.bfloat16), jnp.sin(angle).astype(jnp.bfloat16))


def gaussian(offset):
    return jnp.exp(-0.5 * (offset / smearing) ** 2) / (smearing * math.sqrt(2.0 * math.pi))


def contract_last(left, right):
    return lax.dot_general(
        left, right, (((1,), (1,)), ((), ())), preferred_element_type=jnp.float32
    )


def mixed(form, left, right):
    return jnp.einsum(form, left, right, preferred_element_type=jnp.float32)


def widths(
    bloch_real, bloch_imag, modes, vectors, levels, filled, energy_k, occupation_k, omega, bose
):
    mode_real = modes[:, 0]
    mode_imag = modes[:, 1]
    moded_real = (
        mixed("kqnm,qmv->kqnv", bloch_real, mode_real)
        - mixed("kqnm,qmv->kqnv", bloch_imag, mode_imag)
    ).astype(jnp.bfloat16)
    moded_imag = (
        mixed("kqnm,qmv->kqnv", bloch_real, mode_imag)
        + mixed("kqnm,qmv->kqnv", bloch_imag, mode_real)
    ).astype(jnp.bfloat16)
    vector_real = vectors[:, :, 0]
    vector_imag = vectors[:, :, 1]
    band_real = mixed("qknb,kqnv->kqbv", vector_real, moded_real) + mixed(
        "qknb,kqnv->kqbv", vector_imag, moded_imag
    )
    band_imag = mixed("qknb,kqnv->kqbv", vector_real, moded_imag) - mixed(
        "qknb,kqnv->kqbv", vector_imag, moded_real
    )
    weight = band_real * band_real + band_imag * band_imag
    level_kq = jnp.transpose(levels, (1, 0, 2))[..., None]
    filled_kq = jnp.transpose(filled, (1, 0, 2))[..., None]
    offset = energy_k[:, None, None, None] - level_kq
    freq = omega[None, :, None, :]
    boson = bose[None, :, None, :]
    absorb = gaussian(offset + freq)
    emit = gaussian(offset - freq)
    electron = jnp.sum(
        weight * ((boson + filled_kq) * absorb + (boson + 1.0 - filled_kq) * emit), axis=(1, 2)
    )
    phonon = jnp.sum(weight * (occupation_k[:, None, None, None] - filled_kq) * absorb, axis=(0, 2))
    return (electron, phonon)


MESH = pl.DeviceIdType.MESH
LANES = 128


def bloch_kernel(
    cells_block, tile, last, wq_ref, wk_ref, x_ref, out_ref,
    half, parts, recv, send_sem, recv_sem,
):
    pairs_step = pl.program_id(0)
    cell_step = pl.program_id(1)
    tiles = pl.num_programs(0)
    cell_steps = pl.num_programs(1)
    bands, kas = lax.axis_size("pb"), lax.axis_size("ka")
    devices = bands * kas
    me = lax.axis_index("pb") * kas + lax.axis_index("ka")
    columns = wq_ref.shape[0]
    cells = half.shape[1] // columns
    groups = parts.shape[2]
    mine = groups // bands
    rows = parts.shape[3] // 2
    barrier = pltpu.get_barrier_semaphore()

    @pl.when((pairs_step == 0) & (cell_step == 0))
    def _():
        def greet(step, carry):
            peer = lax.rem(me + step, devices)
            pl.semaphore_signal(
                barrier, inc=1, device_id={"pb": peer // kas, "ka": lax.rem(peer, kas)},
                device_id_type=MESH,
            )
            return carry

        lax.fori_loop(1, devices, greet, 0)

    for cell in range(cells_block):
        right = jnp.concatenate([x_ref[0, cell], x_ref[1, cell]], axis=0)
        product = jnp.dot(wq_ref[...], right, preferred_element_type=jnp.float32)
        row = cell_step * cells_block + cell
        for lane in range(tile // LANES):
            half[lane, pl.ds(row, columns, stride=cells), :] = product[
                :, lane * LANES : (lane + 1) * LANES
            ]

    def strip(index):
        start = pl.multiple_of(index * cells, cells)
        return jnp.concatenate(
            [half[lane, pl.ds(start, cells), :] for lane in range(tile // LANES)], axis=1
        ).astype(jnp.bfloat16)

    @pl.when(cell_step == cell_steps - 1)
    def _():
        def contract(group, carry):
            sums = []
            for member in range(2):
                q = group * 2 + member
                right = jnp.concatenate([strip(q), strip(columns // 2 + q)], axis=0)
                sums.append(
                    jnp.dot(wk_ref[...], right, preferred_element_type=jnp.float32)
                )
            for ka in range(kas):
                block = slice(ka * rows, (ka + 1) * rows)
                parts[pairs_step, ka, group] = jnp.concatenate(
                    [sums[0][block], sums[1][block]], axis=0
                ).astype(jnp.bfloat16)
            return carry

        lax.fori_loop(0, groups, contract, 0, unroll=4)

    @pl.when((cell_step == cell_steps - 1) & (pairs_step == 0))
    def _():
        pl.semaphore_wait(barrier, devices - 1)

    def send(index, width):
        def one(step, carry):
            peer = lax.rem(me + step, devices)
            to_pb, to_ka = peer // kas, lax.rem(peer, kas)
            pltpu.make_async_remote_copy(
                src_ref=parts.at[index, to_ka, pl.ds(to_pb * mine, mine), :, pl.ds(0, width)],
                dst_ref=recv.at[index, me, :, :, pl.ds(0, width)],
                send_sem=send_sem.at[index],
                recv_sem=recv_sem.at[index],
                device_id={"pb": to_pb, "ka": to_ka},
                device_id_type=MESH,
            ).start()
            return carry

        lax.fori_loop(1, devices, one, 0)

    @pl.when((cell_step == cell_steps - 1) & (pairs_step < tiles - 1))
    def _():
        send(pairs_step, tile)

    @pl.when((cell_step == cell_steps - 1) & (pairs_step == tiles - 1))
    def _():
        count = recv.shape[0]
        send(count - 1, last)
        my_pb, my_ka = lax.axis_index("pb"), lax.axis_index("ka")
        for index in range(count):
            recv[index, me] = parts[index, my_ka, pl.ds(my_pb * mine, mine)]
        for index in range(count):
            width = tile if index < count - 1 else last
            window = recv.at[index, pl.ds(1, devices - 1), :, :, pl.ds(0, width)]
            pltpu.make_async_copy(window, window, send_sem.at[index]).wait()
            pltpu.make_async_copy(window, window, recv_sem.at[index]).wait()
            for band in range(bands):
                total = recv[index, band * kas, :, :, :width].astype(jnp.float32)
                for ka in range(1, kas):
                    total = total + recv[index, band * kas + ka, :, :, :width].astype(jnp.float32)
                out_ref[band, :, :, index * tile : index * tile + width] = total.astype(
                    jnp.bfloat16
                )


def bloch(coupling, wq, wk, q_local, k_local):
    bands, kas = lax.axis_size("pb"), lax.axis_size("ka")
    devices = bands * kas
    parts_count, cells, pairs, phonons = coupling.shape
    moved = jnp.transpose(coupling, (0, 1, 3, 2))
    padded = -(-pairs // LANES) * LANES
    if pairs < LANES:
        moved = jnp.pad(moved, ((0, 0), (0, 0), (0, 0), (0, LANES - pairs)))
    tile = min(2 * LANES, padded)
    tiles = -(-padded // tile)
    last = padded - (tiles - 1) * tile
    cells_block = 16
    columns = wq.shape[0]
    groups = columns // 4
    mine = q_local // 2
    rows = 4 * k_local
    result = pl.pallas_call(
        functools.partial(bloch_kernel, cells_block, tile, last),
        grid=(tiles, cells // cells_block),
        in_specs=[
            pl.BlockSpec(wq.shape, lambda t, e: (0, 0)),
            pl.BlockSpec(wk.shape, lambda t, e: (0, 0)),
            pl.BlockSpec((parts_count, cells_block, phonons, tile), lambda t, e: (0, e, 0, t)),
        ],
        out_specs=pl.BlockSpec((bands, mine, rows, padded), lambda t, e: (0, 0, 0, 0)),
        out_shape=jax.ShapeDtypeStruct((bands, mine, rows, padded), jnp.bfloat16),
        scratch_shapes=[
            pltpu.VMEM((tile // LANES, columns * cells, LANES), jnp.float32),
            pltpu.VMEM((tiles, kas, groups, rows, tile), jnp.bfloat16),
            pltpu.VMEM((tiles, devices, mine, rows, tile), jnp.bfloat16),
            pltpu.SemaphoreType.DMA((tiles,)),
            pltpu.SemaphoreType.DMA((tiles,)),
        ],
        compiler_params=pltpu.CompilerParams(
            collective_id=0,
            has_side_effects=True,
            dimension_semantics=("arbitrary", "arbitrary"),
            vmem_limit_bytes=60 * 1024 * 1024,
        ),
        name="bloch",
    )(wq, wk, moved)
    return result[..., :pairs]


def sums_kernel(electron_ref, phonon_ref, electron_out, phonon_out, got_e, got_p, send, recv_e, recv_p):
    bands, kas = lax.axis_size("pb"), lax.axis_size("ka")
    my_pb, my_ka = lax.axis_index("pb"), lax.axis_index("ka")
    barrier = pltpu.get_barrier_semaphore()
    for step in range(1, bands):
        pl.semaphore_signal(
            barrier, inc=1, device_id={"pb": lax.rem(my_pb + step, bands), "ka": my_ka},
            device_id_type=MESH,
        )
    for step in range(1, kas):
        pl.semaphore_signal(
            barrier, inc=1, device_id={"pb": my_pb, "ka": lax.rem(my_ka + step, kas)},
            device_id_type=MESH,
        )
    pl.semaphore_wait(barrier, bands + kas - 2)
    copies = []
    for step in range(1, bands):
        copies.append(pltpu.make_async_remote_copy(
            electron_ref, got_e.at[my_pb], send.at[step - 1], recv_e.at[step - 1],
            device_id={"pb": lax.rem(my_pb + step, bands), "ka": my_ka}, device_id_type=MESH,
        ))
    for step in range(1, kas):
        copies.append(pltpu.make_async_remote_copy(
            phonon_ref, got_p.at[my_ka], send.at[bands + step - 2], recv_p.at[step - 1],
            device_id={"pb": my_pb, "ka": lax.rem(my_ka + step, kas)}, device_id_type=MESH,
        ))
    for copy in copies:
        copy.start()
    got_e[my_pb] = electron_ref[...]
    got_p[my_ka] = phonon_ref[...]
    for copy in copies:
        copy.wait()
    total = got_e[0]
    for step in range(1, bands):
        total = total + got_e[step]
    electron_out[...] = total
    total = got_p[0]
    for step in range(1, kas):
        total = total + got_p[step]
    phonon_out[...] = total


def exchange(electron, phonon):
    bands, kas = lax.axis_size("pb"), lax.axis_size("ka")
    whole = pl.BlockSpec(memory_space=pltpu.VMEM)
    return pl.pallas_call(
        sums_kernel,
        in_specs=[whole, whole],
        out_specs=[whole, whole],
        out_shape=[
            jax.ShapeDtypeStruct(electron.shape, electron.dtype),
            jax.ShapeDtypeStruct(phonon.shape, phonon.dtype),
        ],
        scratch_shapes=[
            pltpu.VMEM((bands, *electron.shape), jnp.float32),
            pltpu.VMEM((kas, *phonon.shape), jnp.float32),
            pltpu.SemaphoreType.DMA((bands + kas - 2,)),
            pltpu.SemaphoreType.DMA((bands - 1,)),
            pltpu.SemaphoreType.DMA((kas - 1,)),
        ],
        compiler_params=pltpu.CompilerParams(collective_id=1, has_side_effects=True),
        name="sums",
    )(electron, phonon)


def angles(points, cells):
    product = lax.dot_general(
        points.astype(jnp.float32).astype(jnp.bfloat16),
        cells.astype(jnp.float32).astype(jnp.bfloat16),
        (((0,), (0,)), ((), ())),
        preferred_element_type=jnp.float32,
    )
    turns = jnp.floor((product + 0.5) * (1.0 / NG))
    angle = (product - turns * NG) * (2.0 * math.pi / NG)
    return jnp.cos(angle), jnp.sin(angle)


def whole_kernel(
    cells_block, tile, last, kpoints, qpoints, electron_cells, phonon_cells, modes, vectors,
    levels, filled, energy_k, occupation_k, omega, bose, x_ref, out_ref,
    wq, wk, half, parts, recv, rows_ref, emission, absorption, totals, got_e, got_p,
    send_sem, recv_sem, send_e, recv_e, send_p, recv_p,
):
    pairs_step = pl.program_id(0)
    cell_step = pl.program_id(1)
    tiles = pl.num_programs(0)
    cell_steps = pl.num_programs(1)
    bands, kas = lax.axis_size("pb"), lax.axis_size("ka")
    devices = bands * kas
    my_pb, my_ka = lax.axis_index("pb"), lax.axis_index("ka")
    me = my_pb * kas + my_ka
    columns = wq.shape[0]
    q_total = columns // 2
    cells = half.shape[1] // columns
    groups = parts.shape[2]
    mine = groups // bands
    rows = parts.shape[3] // 2
    q_local, k_local = vectors.shape[0], vectors.shape[1]
    barrier = pltpu.get_barrier_semaphore()

    @pl.when((pairs_step == 0) & (cell_step == 0))
    def _():
        def greet(step, carry):
            peer = lax.rem(me + step, devices)
            pl.semaphore_signal(
                barrier, inc=1, device_id={"pb": peer // kas, "ka": lax.rem(peer, kas)},
                device_id_type=MESH,
            )
            return carry

        lax.fori_loop(1, devices, greet, 0)
        cos, sin = angles(qpoints[...], phonon_cells[...])
        wq[...] = jnp.concatenate(
            [jnp.concatenate([cos, -sin], 1), jnp.concatenate([sin, cos], 1)], 0
        ).astype(jnp.bfloat16)
        table = electron_cells[...]
        own = table[:, :cells]
        for ka in range(1, kas):
            own = jnp.where(my_ka == ka, table[:, ka * cells : (ka + 1) * cells], own)
        cos, sin = angles(kpoints[...], own)
        blocks = []
        for ka in range(kas):
            c = cos[ka * k_local : (ka + 1) * k_local]
            s = sin[ka * k_local : (ka + 1) * k_local]
            blocks += [jnp.concatenate([c, -s], 1), jnp.concatenate([s, c], 1)]
        wk[...] = jnp.concatenate(blocks, 0).astype(jnp.bfloat16)

    @pl.when((pairs_step == jnp.minimum(tiles - 1, 1)) & (cell_step == 0))
    def _():
        for q in range(q_local):
            freq = omega[q : q + 1, :]
            boson = bose[q : q + 1, :]
            level_q = jnp.transpose(levels[q])
            filled_q = jnp.transpose(filled[q])
            for k in range(k_local):
                f = filled_q[:, k : k + 1]
                offset = energy_k[k] - level_q[:, k : k + 1]
                absorb = gaussian(offset + freq)
                emit = gaussian(offset - freq)
                emission[q, k] = (boson + f) * absorb + (boson + 1.0 - f) * emit
                absorption[q, k] = (occupation_k[k] - f) * absorb

    def project(chunk, carry):
        for step in range(cells_block // 2):
            cell = chunk * (cells_block // 2) + step
            right = jnp.concatenate([x_ref[0, cell], x_ref[1, cell]], axis=0)
            product = jnp.dot(wq[...], right, preferred_element_type=jnp.float32)
            row = cell_step * cells_block + cell
            for lane in range(tile // LANES):
                half[lane, pl.ds(row, columns, stride=cells), :] = product[
                    :, lane * LANES : (lane + 1) * LANES
                ]
        return carry

    lax.fori_loop(0, 2, project, 0)

    def strip(index):
        start = pl.multiple_of(index * cells, cells)
        return jnp.concatenate(
            [half[lane, pl.ds(start, cells), :] for lane in range(tile // LANES)], axis=1
        ).astype(jnp.bfloat16)

    @pl.when(cell_step == cell_steps - 1)
    def _():
        def contract(group, carry):
            sums = []
            for member in range(2):
                q = group * 2 + member
                right = jnp.concatenate([strip(q), strip(q_total + q)], axis=0)
                sums.append(jnp.dot(wk[...], right, preferred_element_type=jnp.float32))
            for ka in range(kas):
                block = slice(ka * rows, (ka + 1) * rows)
                parts[pairs_step, ka, group] = jnp.concatenate(
                    [sums[0][block], sums[1][block]], axis=0
                ).astype(jnp.bfloat16)
            return carry

        lax.fori_loop(0, groups, contract, 0, unroll=4)

    @pl.when((cell_step == cell_steps - 1) & (pairs_step == 0))
    def _():
        pl.semaphore_wait(barrier, devices - 1)

    def send(index, width):
        def one(step, carry):
            peer = lax.rem(me + step, devices)
            to_pb, to_ka = peer // kas, lax.rem(peer, kas)
            pltpu.make_async_remote_copy(
                src_ref=parts.at[index, to_ka, pl.ds(to_pb * mine, mine), :, pl.ds(0, width)],
                dst_ref=recv.at[index, me, :, :, pl.ds(0, width)],
                send_sem=send_sem.at[index],
                recv_sem=recv_sem.at[index],
                device_id={"pb": to_pb, "ka": to_ka},
                device_id_type=MESH,
            ).start()
            return carry

        lax.fori_loop(1, devices, one, 0)

    @pl.when((cell_step == cell_steps - 1) & (pairs_step < tiles - 1))
    def _():
        send(pairs_step, tile)

    @pl.when((cell_step == cell_steps - 1) & (pairs_step == tiles - 1))
    def _():
        count = recv.shape[0]
        send(count - 1, last)
        for index in range(count):
            recv[index, me] = parts[index, my_ka, pl.ds(my_pb * mine, mine)]
        bands_n = rows_ref.shape[0] // (mine * 2 * rows)
        bands_own = bands_n // bands

        def piece(band, group, start):
            stop = start + MODES
            first, final = start // tile, (stop - 1) // tile
            out = []
            for index in range(first, final + 1):
                low, high = max(start, index * tile), min(stop, (index + 1) * tile)
                aligned = (low - index * tile) // LANES * LANES
                upper = -(-(high - index * tile) // LANES) * LANES
                total = recv[index, band * kas, group, :, aligned:upper].astype(jnp.float32)
                for ka in range(1, kas):
                    total = total + recv[
                        index, band * kas + ka, group, :, aligned:upper
                    ].astype(jnp.float32)
                out.append(
                    total[:, low - index * tile - aligned : high - index * tile - aligned]
                )
            return out[0] if len(out) == 1 else jnp.concatenate(out, axis=1)

        for index in range(count):
            width = tile if index < count - 1 else last
            window = recv.at[index, pl.ds(1, devices - 1), :, :, pl.ds(0, width)]
            pltpu.make_async_copy(window, window, recv_sem.at[index]).wait()
            for n in range(bands_own):
                if (n * MODES + MODES - 1) // tile != index:
                    continue
                for band in range(bands):
                    for group in range(mine):
                        row = group * 2 * rows * bands_n + band * bands_own + n
                        rows_ref[pl.ds(row, 2 * rows, stride=bands_n), :MODES] = piece(
                            band, group, n * MODES
                        )
        per_q = rows * bands_n
        side = per_q // 2
        electron = [None] * k_local
        for q in range(q_local):
            left = rows_ref[q * per_q : (q + 1) * per_q, :MODES].astype(jnp.bfloat16)
            by_real = jnp.dot(left, modes[q, 0], preferred_element_type=jnp.float32)
            by_imag = jnp.dot(left, modes[q, 1], preferred_element_type=jnp.float32)
            moded_real = by_real[:side] - by_imag[side:]
            moded_imag = by_imag[:side] + by_real[side:]
            phonon = None
            for k in range(k_local):
                u = jnp.concatenate(
                    [vectors[q, k, 0].astype(jnp.float32), vectors[q, k, 1].astype(jnp.float32)], 0
                ).astype(jnp.bfloat16)
                real = moded_real[k * bands_n : (k + 1) * bands_n]
                imag = moded_imag[k * bands_n : (k + 1) * bands_n]
                over = (((0,), (0,)), ((), ()))
                band_real = lax.dot_general(
                    u, jnp.concatenate([real, imag], 0).astype(jnp.bfloat16), over,
                    preferred_element_type=jnp.float32,
                )
                band_imag = lax.dot_general(
                    u, jnp.concatenate([imag, -real], 0).astype(jnp.bfloat16), over,
                    preferred_element_type=jnp.float32,
                )
                weight = band_real * band_real + band_imag * band_imag
                e_term = weight * emission[q, k]
                p_term = weight * absorption[q, k]
                electron[k] = e_term if q == 0 else electron[k] + e_term
                phonon = p_term if k == 0 else phonon + p_term
            totals[1, q : q + 1, :] = jnp.sum(phonon, axis=0, keepdims=True)
        for k in range(k_local):
            totals[0, k : k + 1, :] = jnp.sum(electron[k], axis=0, keepdims=True)
        copies = []
        for step in range(1, bands):
            copies.append(pltpu.make_async_remote_copy(
                totals.at[0], got_e.at[my_pb], send_e.at[step - 1], recv_e.at[step - 1],
                device_id={"pb": lax.rem(my_pb + step, bands), "ka": my_ka}, device_id_type=MESH,
            ))
        for step in range(1, kas):
            copies.append(pltpu.make_async_remote_copy(
                totals.at[1], got_p.at[my_ka], send_p.at[step - 1], recv_p.at[step - 1],
                device_id={"pb": my_pb, "ka": lax.rem(my_ka + step, kas)}, device_id_type=MESH,
            ))
        for copy in copies:
            copy.start()
        got_e[my_pb] = totals[0]
        got_p[my_ka] = totals[1]
        for index in range(count):
            width = tile if index < count - 1 else last
            window = recv.at[index, pl.ds(1, devices - 1), :, :, pl.ds(0, width)]
            pltpu.make_async_copy(window, window, send_sem.at[index]).wait()
        for copy in copies:
            copy.wait()
        total = got_e[0]
        for step in range(1, bands):
            total = total + got_e[step]
        out_ref[0] = total
        total = got_p[0]
        for step in range(1, kas):
            total = total + got_p[step]
        out_ref[1] = total


def everything(
    coupling, kpoints, qpoints, electron_cells, phonon_cells, phonon_modes, band_vectors,
    energies_kq, occupations_kq, energy_k, occupation_k, frequencies, bose_factors,
):
    bands, kas = lax.axis_size("pb"), lax.axis_size("ka")
    devices = bands * kas
    parts_count, cells, pairs, phonons = coupling.shape
    moved = jnp.transpose(coupling, (0, 1, 3, 2))
    padded = -(-pairs // LANES) * LANES
    tile = LANES
    tiles = -(-padded // tile)
    last = padded - (tiles - 1) * tile
    cells_block = cells
    q_local, k_local = band_vectors.shape[0], band_vectors.shape[1]
    bands_n = band_vectors.shape[3]
    columns = 2 * qpoints.shape[1]
    groups = columns // 4
    mine = q_local // 2
    rows = 2 * k_local
    small = pl.BlockSpec(memory_space=pltpu.VMEM)
    scalars = pl.BlockSpec(memory_space=pltpu.SMEM)
    dma = pltpu.SemaphoreType.DMA
    result = pl.pallas_call(
        functools.partial(whole_kernel, cells_block, tile, last),
        grid=(tiles, cells // cells_block),
        in_specs=[small] * 8
        + [scalars] * 2
        + [small] * 2
        + [pl.BlockSpec((parts_count, cells_block, phonons, tile), lambda t, e: (0, e, 0, t))],
        out_specs=small,
        out_shape=jax.ShapeDtypeStruct((2, k_local, MODES), jnp.float32),
        scratch_shapes=[
            pltpu.VMEM((columns, 2 * phonons), jnp.bfloat16),
            pltpu.VMEM((2 * k_local * kas, 2 * cells), jnp.bfloat16),
            pltpu.VMEM((tile // LANES, columns * cells, LANES), jnp.float32),
            pltpu.VMEM((tiles, kas, groups, 2 * rows, tile), jnp.bfloat16),
            pltpu.VMEM((tiles, devices, mine, 2 * rows, tile), jnp.bfloat16),
            pltpu.VMEM((q_local * rows * bands_n, LANES), jnp.float32),
            pltpu.VMEM((q_local, k_local, bands_n, MODES), jnp.float32),
            pltpu.VMEM((q_local, k_local, bands_n, MODES), jnp.float32),
            pltpu.VMEM((2, k_local, MODES), jnp.float32),
            pltpu.VMEM((bands, k_local, MODES), jnp.float32),
            pltpu.VMEM((kas, k_local, MODES), jnp.float32),
            dma((tiles,)),
            dma((tiles,)),
            dma((bands - 1,)),
            dma((bands - 1,)),
            dma((kas - 1,)),
            dma((kas - 1,)),
        ],
        compiler_params=pltpu.CompilerParams(
            collective_id=2,
            has_side_effects=True,
            dimension_semantics=("arbitrary", "arbitrary"),
            vmem_limit_bytes=60 * 1024 * 1024,
        ),
        name="widths",
    )(
        kpoints, qpoints, electron_cells, phonon_cells, phonon_modes, band_vectors, energies_kq,
        occupations_kq, energy_k, occupation_k, frequencies, bose_factors, moved,
    )
    return result


def on_device(
    coupling,
    kpoints,
    qpoints,
    electron_cells,
    phonon_cells,
    phonon_modes,
    band_vectors,
    energies_kq,
    occupations_kq,
    energy_k,
    occupation_k,
    frequencies,
    bose_factors,
):
    k_local = energy_k.shape[0]
    q_local = frequencies.shape[0]
    cells_local = coupling.shape[1]
    bands, kas = lax.axis_size("pb"), lax.axis_size("ka")
    q_total = q_local * bands
    k_total = k_local * kas
    if coupling.shape[2] % MODES == 0 and k_local == q_local:
        sums = everything(
            coupling, kpoints, qpoints, electron_cells, phonon_cells, phonon_modes, band_vectors,
            energies_kq, occupations_kq, energy_k, occupation_k, frequencies, bose_factors,
        )
        return (sums[0] / (q_total * NB), sums[1] / (k_total * NB))
    cos_q, sin_q = phase_table(qpoints, phonon_cells)
    own_cells = lax.dynamic_slice_in_dim(
        electron_cells, lax.axis_index("ka") * cells_local, cells_local, 1
    )
    cos_k, sin_k = phase_table(kpoints, own_cells)
    wq = jnp.concatenate(
        [jnp.concatenate([cos_q, -sin_q], 1), jnp.concatenate([sin_q, cos_q], 1)], 0
    )
    wk = jnp.stack(
        [jnp.concatenate([cos_k, -sin_k], 1), jnp.concatenate([sin_k, cos_k], 1)], 1
    ).reshape(2 * k_total, 2 * cells_local)
    values = bloch(coupling, wq, wk, q_local, k_local)
    values = values.reshape(bands, q_local // 2, 2, k_local, 2, -1)
    values = jnp.transpose(values, (4, 3, 1, 2, 0, 5)).reshape(2, k_local, q_local, NB, MODES)
    electron, phonon = widths(
        values[0],
        values[1],
        phonon_modes,
        band_vectors,
        energies_kq,
        occupations_kq,
        energy_k,
        occupation_k,
        frequencies,
        bose_factors,
    )
    electron_width, phonon_width = exchange(electron / (q_total * NB), phonon / (k_total * NB))
    return (electron_width, phonon_width)


def solution(mesh):
    in_specs = (
        P(None, "ka", "pb", None),
        P(),
        P(),
        P(),
        P(),
        P("pb", None, None, None),
        P("pb", "ka", None, None, None),
        P("pb", "ka", None),
        P("pb", "ka", None),
        P("ka"),
        P("ka"),
        P("pb", None),
        P("pb", None),
    )
    out_specs = (P("ka", None), P("pb", None))
    return jax.shard_map(
        on_device, mesh=mesh, in_specs=in_specs, out_specs=out_specs, check_vma=False
    )
```

profile of v0, /device:TPU:0, one launch (start us, length us, event | category | flops | bytes accessed | tf_op | source)
XLA Modules:
  0.0 50.7 jit_solution(73883750027244510)
XLA Ops:
  0.6 48.8 %widths.1 = f32[2,4,120]{2,1,0:T(4,128)} custom-call(s32[3,16]{1,0:T(4,128)} %kpoints.1, s32[3,32]{1,0:T(4,128)} %qpoints.1, s32[3,320]{1,0:T(4,128)} %electron_cells.1, s32[3,320]{1,0:T(4,128)} %phonon_cells.1, bf16[4,2,120,120]{3,2,1,0:T(8,128)(2,1)} %modes.1, bf16[4,4,2,40,40]{4,3,2,1,0:T(8,128)(2,1)} %vectors.1, f32[4,4,40]{2,1,0:T(4,128)} %levels.1, ...), custom_call_target="tpu_custom_call" | custom-call | tf_op jit(solution)/shard_map/widths/pallas_call | solution.py:565
  49.4 1.3 %multiply_bitcast_fusion = (f32[4,120]{1,0:T(4,128)}, f32[4,120]{1,0:T(4,128)}) fusion(f32[2,4,120]{2,1,0:T(4,128)} %widths.1), kind=kLoop, calls=%fused_computation | loop fusion | flops 960 | bytes 7680 | tf_op jit(solution)/shard_map/div | solution.py:633
where the time goes:
time: 50.9 us; the launch traced here: 50.7 us
  Pallas kernels  48.8 us (96%)
  other arithmetic  1.26 us (2%)
  between operations  0.64 us (1%)
    pallas_call x1, Pallas kernels, everything(): pl.pallas_call(functools.partial(whole_kernel, cells_block, tile, last),...  48.8 us
    div x1, other arithmetic, on_device(): return (sums[0] / (q_total * NB), sums[1] / (k_total * NB))  1.26 us

commit v1 on v0

--- a/solution.py
+++ b/solution.py
@@ -310,33 +310,134 @@
     return jnp.cos(angle), jnp.sin(angle)
 
 
-def whole_kernel(
-    cells_block, tile, last, kpoints, qpoints, electron_cells, phonon_cells, modes, vectors,
-    levels, filled, energy_k, occupation_k, omega, bose, x_ref, out_ref,
-    wq, wk, half, parts, recv, rows_ref, emission, absorption, totals, got_e, got_p,
-    send_sem, recv_sem, send_e, recv_e, send_p, recv_p,
+def ring_kernel(
+    pairs, kpoints, qpoints, electron_cells, phonon_cells, modes, vectors,
+    levels, filled, energy_k, occupation_k, omega, bose, edge_ref, x_hbm, out_ref,
+    wq, wk, half, ring, parts, recv, relay, sums, table, lifted, rows_ref, turned,
+    emission, absorption, totals, got_e, got_p,
+    ring_sem, relay_send, relay_recv, plane_send, plane_recv, raw_send, raw_recv,
+    sum_send, sum_recv, send_e, recv_e, send_p, recv_p,
 ):
-    pairs_step = pl.program_id(0)
-    cell_step = pl.program_id(1)
-    tiles = pl.num_programs(0)
-    cell_steps = pl.num_programs(1)
+    step = pl.program_id(0)
+    steps = pl.num_programs(0)
     bands, kas = lax.axis_size("pb"), lax.axis_size("ka")
     devices = bands * kas
     my_pb, my_ka = lax.axis_index("pb"), lax.axis_index("ka")
     me = my_pb * kas + my_ka
     columns = wq.shape[0]
     q_total = columns // 2
-    cells = half.shape[1] // columns
-    groups = parts.shape[2]
-    mine = groups // bands
-    rows = parts.shape[3] // 2
+    cells = half.shape[0] // columns
+    slots, unit = ring.shape[0], ring.shape[2]
+    chunks = cells // unit
+    tiles = parts.shape[0]
+    halves = parts.shape[3]
+    mine = 2 * halves
     q_local, k_local = vectors.shape[0], vectors.shape[1]
+    rows = 2 * k_local
+    bands_n = vectors.shape[3]
+    bands_own = bands_n // bands
+    up, down = lax.rem(my_ka + 1, kas), lax.rem(my_ka + kas - 1, kas)
+    across = lax.rem(my_ka + 2, kas)
     barrier = pltpu.get_barrier_semaphore()
-
-    @pl.when((pairs_step == 0) & (cell_step == 0))
+    overlaps = []
+    for tile in range(tiles):
+        for n in range(bands_own):
+            low = max(tile * LANES, n * MODES)
+            high = min((tile + 1) * LANES, (n + 1) * MODES)
+            if low < high:
+                overlaps.append((tile, n, low - tile * LANES, low - n * MODES, high - low))
+
+    def fetch(index, slot):
+        tile, chunk = index // chunks, lax.rem(index, chunks)
+        return pltpu.make_async_copy(
+            x_hbm.at[
+                :, pl.ds(chunk * unit, unit), :, pl.ds(pl.multiple_of(tile * LANES, LANES), LANES)
+            ],
+            ring.at[slot],
+            ring_sem.at[slot],
+        )
+
+    def project(real, imag, row):
+        right = jnp.concatenate([real, imag], axis=0)
+        product = jnp.dot(wq[...], right, preferred_element_type=jnp.float32)
+        half[pl.ds(row, columns, stride=cells), :] = product
+
+    def strip(index):
+        return half[index * cells : (index + 1) * cells, :].astype(jnp.bfloat16)
+
+    def contract(order):
+        for group in range(q_total // 2):
+            products = []
+            for member in range(2):
+                q = group * 2 + member
+                right = jnp.concatenate([strip(q), strip(q_total + q)], axis=0)
+                products.append(jnp.dot(wk[...], right, preferred_element_type=jnp.float32))
+            m = group % mine
+            for ka in range(kas):
+                block = slice(ka * rows, (ka + 1) * rows)
+                parts[order, ka, m // halves, m % halves, group // mine] = jnp.concatenate(
+                    [products[0][block], products[1][block]], axis=0
+                ).astype(jnp.bfloat16)
+
+    def put(source, target, send_sem, recv_sem, to_pb, to_ka):
+        pltpu.make_async_remote_copy(
+            src_ref=source, dst_ref=target, send_sem=send_sem, recv_sem=recv_sem,
+            device_id={"pb": to_pb, "ka": to_ka}, device_id_type=MESH,
+        ).start()
+
+    def settle(window, sem):
+        pltpu.make_async_copy(window, window, sem).wait()
+
+    def send(order):
+        put(parts.at[order, across, 0], relay.at[order, 0], relay_send.at[0, order],
+            relay_recv.at[0, order], my_pb, up)
+        put(parts.at[order, across, 1], relay.at[order, 1], relay_send.at[1, order],
+            relay_recv.at[1, order], my_pb, down)
+
+        def raw(index, carry):
+            to = lax.rem(my_pb + index, bands)
+            put(parts.at[order, up, 1, :, to], recv.at[order, 1, 1, :, my_pb],
+                raw_send.at[0, order], raw_recv.at[0, order], to, up)
+            put(parts.at[order, down, 0, :, to], recv.at[order, 2, 0, :, my_pb],
+                raw_send.at[1, order], raw_recv.at[1, order], to, down)
+            return carry
+
+        lax.fori_loop(0, bands, raw, 0)
+
+        def plane(index, carry):
+            to = lax.rem(my_pb + index, bands)
+            put(parts.at[order, my_ka, :, :, to], recv.at[order, 0, :, :, my_pb],
+                plane_send.at[order], plane_recv.at[order], to, my_ka)
+            return carry
+
+        lax.fori_loop(1, bands, plane, 0)
+
+    def pass_on(order):
+        for way, (target, place) in enumerate(((up, 1), (down, 2))):
+            settle(relay.at[order, way], relay_recv.at[way, order])
+            own = parts[order, target, way].astype(jnp.float32)
+            sums[order, way] = (own + relay[order, way].astype(jnp.float32)).astype(jnp.bfloat16)
+
+            def one(index, carry, way=way, target=target, place=place):
+                to = lax.rem(my_pb + index, bands)
+                put(sums.at[order, way, :, to], recv.at[order, place, way, :, my_pb],
+                    sum_send.at[way, order], sum_recv.at[way, order], to, target)
+                return carry
+
+            lax.fori_loop(0, bands, one, 0)
+
+    edge_cells = edge_ref.shape[1]
+
+    def edge(index, carry):
+        for inner in range(unit):
+            cell = index * unit + inner
+            project(edge_ref[0, cell], edge_ref[1, cell], step * edge_cells + cell)
+        return carry
+
+    @pl.when(step == 0)
     def _():
-        def greet(step, carry):
-            peer = lax.rem(me + step, devices)
+        def greet(index, carry):
+            peer = lax.rem(me + index, devices)
             pl.semaphore_signal(
                 barrier, inc=1, device_id={"pb": peer // kas, "ka": lax.rem(peer, kas)},
                 device_id_type=MESH,
@@ -344,14 +445,20 @@
             return carry
 
         lax.fori_loop(1, devices, greet, 0)
+
+        def first(index, carry):
+            fetch(index, index).start()
+            return carry
+
+        lax.fori_loop(0, slots, first, 0)
         cos, sin = angles(qpoints[...], phonon_cells[...])
         wq[...] = jnp.concatenate(
             [jnp.concatenate([cos, -sin], 1), jnp.concatenate([sin, cos], 1)], 0
         ).astype(jnp.bfloat16)
-        table = electron_cells[...]
-        own = table[:, :cells]
+        cells_all = electron_cells[...]
+        own = cells_all[:, :cells]
         for ka in range(1, kas):
-            own = jnp.where(my_ka == ka, table[:, ka * cells : (ka + 1) * cells], own)
+            own = jnp.where(my_ka == ka, cells_all[:, ka * cells : (ka + 1) * cells], own)
         cos, sin = angles(kpoints[...], own)
         blocks = []
         for ka in range(kas):
@@ -360,7 +467,9 @@
             blocks += [jnp.concatenate([c, -s], 1), jnp.concatenate([s, c], 1)]
         wk[...] = jnp.concatenate(blocks, 0).astype(jnp.bfloat16)
 
-    @pl.when((pairs_step == jnp.minimum(tiles - 1, 1)) & (cell_step == 0))
+    lax.fori_loop(0, edge_cells // unit, edge, 0)
+
+    @pl.when(step == 0)
     def _():
         for q in range(q_local):
             freq = omega[q : q + 1, :]
@@ -374,133 +483,120 @@
                 emit = gaussian(offset - freq)
                 emission[q, k] = (boson + f) * absorb + (boson + 1.0 - f) * emit
                 absorption[q, k] = (occupation_k[k] - f) * absorb
-
-    def project(chunk, carry):
-        for step in range(cells_block // 2):
-            cell = chunk * (cells_block // 2) + step
-            right = jnp.concatenate([x_ref[0, cell], x_ref[1, cell]], axis=0)
-            product = jnp.dot(wq[...], right, preferred_element_type=jnp.float32)
-            row = cell_step * cells_block + cell
-            for lane in range(tile // LANES):
-                half[lane, pl.ds(row, columns, stride=cells), :] = product[
-                    :, lane * LANES : (lane + 1) * LANES
+                for part in range(2):
+                    rows_ref[part, :, :bands_n] = vectors[q, k, part].astype(jnp.float32)
+                real, imag = (
+                    jnp.concatenate(
+                        [
+                            rows_ref[part, pl.ds(n, bands, stride=bands_own), :]
+                            for n in range(bands_own)
+                        ],
+                        axis=0,
+                    )[:, :bands_n]
+                    for part in range(2)
+                )
+                both = jnp.concatenate(
+                    [jnp.concatenate([real, -imag], 1), jnp.concatenate([imag, real], 1)], 0
+                )
+                turned[q, k] = jnp.transpose(both).astype(jnp.bfloat16)
+            for part in range(2):
+                mode = modes[q, part].astype(jnp.float32)
+                for index, (tile, n, row, start, count) in enumerate(overlaps):
+                    pieces = []
+                    if row:
+                        pieces.append(jnp.zeros((row, MODES), jnp.float32))
+                    pieces.append(mode[start : start + count])
+                    if row + count < LANES:
+                        pieces.append(jnp.zeros((LANES - row - count, MODES), jnp.float32))
+                    placed = jnp.concatenate(pieces, 0) if len(pieces) > 1 else pieces[0]
+                    table[q, index, :, part * LANES : part * LANES + MODES] = placed.astype(
+                        jnp.bfloat16
+                    )
+
+    @pl.when(step == steps - 1)
+    def _():
+        contract(0)
+        pl.semaphore_wait(barrier, devices - 1)
+        send(0)
+
+        def one_tile(tile, carry):
+            def one_chunk(chunk, inner_carry):
+                index = tile * chunks + chunk
+                slot = lax.rem(index, slots)
+                fetch(index, slot).wait()
+                for inner in range(unit):
+                    project(ring[slot, 0, inner], ring[slot, 1, inner], chunk * unit + inner)
+
+                @pl.when(index + slots < (tiles - 1) * chunks)
+                def _():
+                    fetch(index + slots, slot).start()
+
+                return inner_carry
+
+            lax.fori_loop(0, chunks, one_chunk, 0)
+            contract(tile + 1)
+            send(tile + 1)
+            pass_on(tile)
+            return carry
+
+        lax.fori_loop(0, tiles - 1, one_tile, 0)
+        for order in range(tiles):
+            recv[order, 0, :, :, my_pb] = parts[order, my_ka, :, :, my_pb]
+        pass_on(tiles - 1)
+        lane = lax.broadcasted_iota(jnp.int32, (1, LANES), 1)
+        started = set()
+        for order in range(tiles):
+            tile = tiles - 1 if order == 0 else order - 1
+            settle(recv.at[order, 0, :, :, pl.ds(1, bands - 1)], plane_recv.at[order])
+            for way in range(2):
+                settle(recv.at[order, 1 + way, 1 - way], raw_recv.at[way, order])
+            for way in range(2):
+                settle(recv.at[order, 1 + way, way], sum_recv.at[way, order])
+            for m in range(mine):
+                spot = (m // halves, m % halves)
+                total = [
+                    recv[order, 0, *spot, band].astype(jnp.float32)
+                    + recv[order, 1, *spot, band].astype(jnp.float32)
+                    + recv[order, 2, *spot, band].astype(jnp.float32)
+                    for band in range(bands)
                 ]
-        return carry
-
-    lax.fori_loop(0, 2, project, 0)
-
-    def strip(index):
-        start = pl.multiple_of(index * cells, cells)
-        return jnp.concatenate(
-            [half[lane, pl.ds(start, cells), :] for lane in range(tile // LANES)], axis=1
-        ).astype(jnp.bfloat16)
-
-    @pl.when(cell_step == cell_steps - 1)
-    def _():
-        def contract(group, carry):
-            sums = []
-            for member in range(2):
-                q = group * 2 + member
-                right = jnp.concatenate([strip(q), strip(q_total + q)], axis=0)
-                sums.append(jnp.dot(wk[...], right, preferred_element_type=jnp.float32))
-            for ka in range(kas):
-                block = slice(ka * rows, (ka + 1) * rows)
-                parts[pairs_step, ka, group] = jnp.concatenate(
-                    [sums[0][block], sums[1][block]], axis=0
-                ).astype(jnp.bfloat16)
-            return carry
-
-        lax.fori_loop(0, groups, contract, 0, unroll=4)
-
-    @pl.when((cell_step == cell_steps - 1) & (pairs_step == 0))
-    def _():
-        pl.semaphore_wait(barrier, devices - 1)
-
-    def send(index, width):
-        def one(step, carry):
-            peer = lax.rem(me + step, devices)
-            to_pb, to_ka = peer // kas, lax.rem(peer, kas)
-            pltpu.make_async_remote_copy(
-                src_ref=parts.at[index, to_ka, pl.ds(to_pb * mine, mine), :, pl.ds(0, width)],
-                dst_ref=recv.at[index, me, :, :, pl.ds(0, width)],
-                send_sem=send_sem.at[index],
-                recv_sem=recv_sem.at[index],
-                device_id={"pb": to_pb, "ka": to_ka},
-                device_id_type=MESH,
-            ).start()
-            return carry
-
-        lax.fori_loop(1, devices, one, 0)
-
-    @pl.when((cell_step == cell_steps - 1) & (pairs_step < tiles - 1))
-    def _():
-        send(pairs_step, tile)
-
-    @pl.when((cell_step == cell_steps - 1) & (pairs_step == tiles - 1))
-    def _():
-        count = recv.shape[0]
-        send(count - 1, last)
-        for index in range(count):
-            recv[index, me] = parts[index, my_ka, pl.ds(my_pb * mine, mine)]
-        bands_n = rows_ref.shape[0] // (mine * 2 * rows)
-        bands_own = bands_n // bands
-
-        def piece(band, group, start):
-            stop = start + MODES
-            first, final = start // tile, (stop - 1) // tile
-            out = []
-            for index in range(first, final + 1):
-                low, high = max(start, index * tile), min(stop, (index + 1) * tile)
-                aligned = (low - index * tile) // LANES * LANES
-                upper = -(-(high - index * tile) // LANES) * LANES
-                total = recv[index, band * kas, group, :, aligned:upper].astype(jnp.float32)
-                for ka in range(1, kas):
-                    total = total + recv[
-                        index, band * kas + ka, group, :, aligned:upper
-                    ].astype(jnp.float32)
-                out.append(
-                    total[:, low - index * tile - aligned : high - index * tile - aligned]
-                )
-            return out[0] if len(out) == 1 else jnp.concatenate(out, axis=1)
-
-        for index in range(count):
-            width = tile if index < count - 1 else last
-            window = recv.at[index, pl.ds(1, devices - 1), :, :, pl.ds(0, width)]
-            pltpu.make_async_copy(window, window, recv_sem.at[index]).wait()
-            for n in range(bands_own):
-                if (n * MODES + MODES - 1) // tile != index:
-                    continue
-                for band in range(bands):
-                    for group in range(mine):
-                        row = group * 2 * rows * bands_n + band * bands_own + n
-                        rows_ref[pl.ds(row, 2 * rows, stride=bands_n), :MODES] = piece(
-                            band, group, n * MODES
+                for member in range(2):
+                    q = 2 * m + member
+                    left = jnp.concatenate(
+                        [one[member * rows : (member + 1) * rows] for one in total], axis=0
+                    )
+                    if pairs < (tile + 1) * LANES:
+                        left = jnp.where(lane < pairs - tile * LANES, left, 0.0)
+                    left = left.astype(jnp.bfloat16)
+                    for index, (other, n, _, _, _) in enumerate(overlaps):
+                        if other != tile:
+                            continue
+                        product = jnp.dot(
+                            left, table[q, index], preferred_element_type=jnp.float32
                         )
-        per_q = rows * bands_n
-        side = per_q // 2
+                        for side in range(2):
+                            value = product[:, side * LANES : (side + 1) * LANES]
+                            if (q, n) in started:
+                                value = value + lifted[q, n, side]
+                            lifted[q, n, side] = value
+                        started.add((q, n))
         electron = [None] * k_local
         for q in range(q_local):
-            left = rows_ref[q * per_q : (q + 1) * per_q, :MODES].astype(jnp.bfloat16)
-            by_real = jnp.dot(left, modes[q, 0], preferred_element_type=jnp.float32)
-            by_imag = jnp.dot(left, modes[q, 1], preferred_element_type=jnp.float32)
-            moded_real = by_real[:side] - by_imag[side:]
-            moded_imag = by_imag[:side] + by_real[side:]
             phonon = None
             for k in range(k_local):
-                u = jnp.concatenate(
-                    [vectors[q, k, 0].astype(jnp.float32), vectors[q, k, 1].astype(jnp.float32)], 0
-                ).astype(jnp.bfloat16)
-                real = moded_real[k * bands_n : (k + 1) * bands_n]
-                imag = moded_imag[k * bands_n : (k + 1) * bands_n]
-                over = (((0,), (0,)), ((), ()))
-                band_real = lax.dot_general(
-                    u, jnp.concatenate([real, imag], 0).astype(jnp.bfloat16), over,
-                    preferred_element_type=jnp.float32,
-                )
-                band_imag = lax.dot_general(
-                    u, jnp.concatenate([imag, -real], 0).astype(jnp.bfloat16), over,
-                    preferred_element_type=jnp.float32,
-                )
+                real, imag = [], []
+                for n in range(bands_own):
+                    rr, ri, ir, ii = (
+                        lifted[q, n, side, pl.ds(part * k_local + k, bands, stride=rows), :]
+                        for part in range(2)
+                        for side in range(2)
+                    )
+                    real.append(rr - ii)
+                    imag.append(ri + ir)
+                right = jnp.concatenate(real + imag, axis=0).astype(jnp.bfloat16)
+                band = jnp.dot(turned[q, k], right, preferred_element_type=jnp.float32)
+                band_real = band[:bands_n, :MODES]
+                band_imag = band[bands_n:, :MODES]
                 weight = band_real * band_real + band_imag * band_imag
                 e_term = weight * emission[q, k]
                 p_term = weight * absorption[q, k]
@@ -510,33 +606,35 @@
         for k in range(k_local):
             totals[0, k : k + 1, :] = jnp.sum(electron[k], axis=0, keepdims=True)
         copies = []
-        for step in range(1, bands):
+        for shift in range(1, bands):
             copies.append(pltpu.make_async_remote_copy(
-                totals.at[0], got_e.at[my_pb], send_e.at[step - 1], recv_e.at[step - 1],
-                device_id={"pb": lax.rem(my_pb + step, bands), "ka": my_ka}, device_id_type=MESH,
+                totals.at[0], got_e.at[my_pb], send_e.at[shift - 1], recv_e.at[shift - 1],
+                device_id={"pb": lax.rem(my_pb + shift, bands), "ka": my_ka}, device_id_type=MESH,
             ))
-        for step in range(1, kas):
+        for shift in range(1, kas):
             copies.append(pltpu.make_async_remote_copy(
-                totals.at[1], got_p.at[my_ka], send_p.at[step - 1], recv_p.at[step - 1],
-                device_id={"pb": my_pb, "ka": lax.rem(my_ka + step, kas)}, device_id_type=MESH,
+                totals.at[1], got_p.at[my_ka], send_p.at[shift - 1], recv_p.at[shift - 1],
+                device_id={"pb": my_pb, "ka": lax.rem(my_ka + shift, kas)}, device_id_type=MESH,
             ))
         for copy in copies:
             copy.start()
         got_e[my_pb] = totals[0]
         got_p[my_ka] = totals[1]
-        for index in range(count):
-            width = tile if index < count - 1 else last
-            window = recv.at[index, pl.ds(1, devices - 1), :, :, pl.ds(0, width)]
-            pltpu.make_async_copy(window, window, send_sem.at[index]).wait()
+        for order in range(tiles):
+            settle(recv.at[order, 0, :, :, pl.ds(1, bands - 1)], plane_send.at[order])
+            for way in range(2):
+                settle(relay.at[order, way], relay_send.at[way, order])
+                settle(recv.at[order, 1 + way, 1 - way], raw_send.at[way, order])
+                settle(recv.at[order, 1 + way, way], sum_send.at[way, order])
         for copy in copies:
             copy.wait()
         total = got_e[0]
-        for step in range(1, bands):
-            total = total + got_e[step]
+        for other in range(1, bands):
+            total = total + got_e[other]
         out_ref[0] = total
         total = got_p[0]
-        for step in range(1, kas):
-            total = total + got_p[step]
+        for other in range(1, kas):
+            total = total + got_p[other]
         out_ref[1] = total
 
 
@@ -545,46 +643,65 @@
     energies_kq, occupations_kq, energy_k, occupation_k, frequencies, bose_factors,
 ):
     bands, kas = lax.axis_size("pb"), lax.axis_size("ka")
-    devices = bands * kas
     parts_count, cells, pairs, phonons = coupling.shape
     moved = jnp.transpose(coupling, (0, 1, 3, 2))
-    padded = -(-pairs // LANES) * LANES
-    tile = LANES
-    tiles = -(-padded // tile)
-    last = padded - (tiles - 1) * tile
-    cells_block = cells
+    tiles = -(-pairs // LANES)
+    unit = cells // 4
+    slots = 8
     q_local, k_local = band_vectors.shape[0], band_vectors.shape[1]
     bands_n = band_vectors.shape[3]
     columns = 2 * qpoints.shape[1]
-    groups = columns // 4
-    mine = q_local // 2
-    rows = 2 * k_local
+    halves = q_local // 4
+    rows = 4 * k_local
+    bands_own = bands_n // bands
+    overlaps = sum(
+        max(t * LANES, n * MODES) < min((t + 1) * LANES, (n + 1) * MODES)
+        for t in range(tiles)
+        for n in range(bands_own)
+    )
     small = pl.BlockSpec(memory_space=pltpu.VMEM)
     scalars = pl.BlockSpec(memory_space=pltpu.SMEM)
     dma = pltpu.SemaphoreType.DMA
-    result = pl.pallas_call(
-        functools.partial(whole_kernel, cells_block, tile, last),
-        grid=(tiles, cells // cells_block),
+    bf16, f32 = jnp.bfloat16, jnp.float32
+    return pl.pallas_call(
+        functools.partial(ring_kernel, pairs),
+        grid=(2,),
         in_specs=[small] * 8
         + [scalars] * 2
         + [small] * 2
-        + [pl.BlockSpec((parts_count, cells_block, phonons, tile), lambda t, e: (0, e, 0, t))],
+        + [
+            pl.BlockSpec((parts_count, cells // 2, phonons, LANES), lambda e: (0, e, 0, tiles - 1)),
+            pl.BlockSpec(memory_space=pl.ANY),
+        ],
         out_specs=small,
-        out_shape=jax.ShapeDtypeStruct((2, k_local, MODES), jnp.float32),
+        out_shape=jax.ShapeDtypeStruct((2, k_local, MODES), f32),
         scratch_shapes=[
-            pltpu.VMEM((columns, 2 * phonons), jnp.bfloat16),
-            pltpu.VMEM((2 * k_local * kas, 2 * cells), jnp.bfloat16),
-            pltpu.VMEM((tile // LANES, columns * cells, LANES), jnp.float32),
-            pltpu.VMEM((tiles, kas, groups, 2 * rows, tile), jnp.bfloat16),
-            pltpu.VMEM((tiles, devices, mine, 2 * rows, tile), jnp.bfloat16),
-            pltpu.VMEM((q_local * rows * bands_n, LANES), jnp.float32),
-            pltpu.VMEM((q_local, k_local, bands_n, MODES), jnp.float32),
-            pltpu.VMEM((q_local, k_local, bands_n, MODES), jnp.float32),
-            pltpu.VMEM((2, k_local, MODES), jnp.float32),
-            pltpu.VMEM((bands, k_local, MODES), jnp.float32),
-            pltpu.VMEM((kas, k_local, MODES), jnp.float32),
+            pltpu.VMEM((columns, 2 * phonons), bf16),
+            pltpu.VMEM((2 * k_local * kas, 2 * cells), bf16),
+            pltpu.VMEM((columns * cells, LANES), f32),
+            pltpu.VMEM((slots, parts_count, unit, phonons, LANES), bf16),
+            pltpu.VMEM((tiles, kas, 2, halves, bands, rows, LANES), bf16),
+            pltpu.VMEM((tiles, 3, 2, halves, bands, rows, LANES), bf16),
+            pltpu.VMEM((tiles, 2, halves, bands, rows, LANES), bf16),
+            pltpu.VMEM((tiles, 2, halves, bands, rows, LANES), bf16),
+            pltpu.VMEM((q_local, overlaps, LANES, 2 * LANES), bf16),
+            pltpu.VMEM((q_local, bands_own, 2, bands * 2 * k_local, LANES), f32),
+            pltpu.VMEM((2, bands_n, LANES), f32),
+            pltpu.VMEM((q_local, k_local, 2 * bands_n, 2 * bands_n), bf16),
+            pltpu.VMEM((q_local, k_local, bands_n, MODES), f32),
+            pltpu.VMEM((q_local, k_local, bands_n, MODES), f32),
+            pltpu.VMEM((2, k_local, MODES), f32),
+            pltpu.VMEM((bands, k_local, MODES), f32),
+            pltpu.VMEM((kas, k_local, MODES), f32),
+            dma((slots,)),
+            dma((2, tiles)),
+            dma((2, tiles)),
             dma((tiles,)),
             dma((tiles,)),
+            dma((2, tiles)),
+            dma((2, tiles)),
+            dma((2, tiles)),
+            dma((2, tiles)),
             dma((bands - 1,)),
             dma((bands - 1,)),
             dma((kas - 1,)),
@@ -593,15 +710,14 @@
         compiler_params=pltpu.CompilerParams(
             collective_id=2,
             has_side_effects=True,
-            dimension_semantics=("arbitrary", "arbitrary"),
+            dimension_semantics=("arbitrary",),
             vmem_limit_bytes=60 * 1024 * 1024,
         ),
         name="widths",
     )(
         kpoints, qpoints, electron_cells, phonon_cells, phonon_modes, band_vectors, energies_kq,
-        occupations_kq, energy_k, occupation_k, frequencies, bose_factors, moved,
-    )
-    return result
+        occupations_kq, energy_k, occupation_k, frequencies, bose_factors, moved, moved,
+    )
 
 
 def on_device(
@@ -625,7 +741,9 @@
     bands, kas = lax.axis_size("pb"), lax.axis_size("ka")
     q_total = q_local * bands
     k_total = k_local * kas
-    if coupling.shape[2] % MODES == 0 and k_local == q_local:
+    whole_bands = coupling.shape[2] % MODES == 0 and coupling.shape[2] > LANES
+    even = q_local % 4 == 0 and cells_local % 16 == 0
+    if kas == 4 and whole_bands and even and k_local == q_local:
         sums = everything(
             coupling, kpoints, qpoints, electron_cells, phonon_cells, phonon_modes, band_vectors,
             energies_kq, occupations_kq, energy_k, occupation_k, frequencies, bose_factors,

time: 50.9 us -> 47.5 us (0.933)
  Pallas kernels: 48.8 us -> 45.4 us
    pallas_call x1, Pallas kernels: 48.8 us -> 45.4 us  [everything(): pl.pallas_call(functools.partial(ring_kernel, pairs), grid=(2,), in_specs...]
where the time goes in v1:
time: 47.5 us; the launch traced here: 47.3 us
  Pallas kernels  45.4 us (96%)
  other arithmetic  1.26 us (3%)
  between operations  0.64 us (1%)
    pallas_call x1, Pallas kernels, everything(): pl.pallas_call(functools.partial(ring_kernel, pairs), grid=(2,), in_specs...  45.4 us
    div x1, other arithmetic, on_device(): return (sums[0] / (q_total * NB), sums[1] / (k_total * NB))  1.26 us

profile of v1, /device:TPU:0, one launch (start us, length us, event | category | flops | bytes accessed | tf_op | source)
XLA Modules:
  0.0 47.3 jit_solution(16272463317881956682)
XLA Ops:
  0.6 45.4 %widths.1 = f32[2,4,120]{2,1,0:T(4,128)} custom-call(s32[3,16]{1,0:T(4,128)} %kpoints.1, s32[3,32]{1,0:T(4,128)} %qpoints.1, s32[3,320]{1,0:T(4,128)} %electron_cells.1, s32[3,320]{1,0:T(4,128)} %phonon_cells.1, bf16[4,2,120,120]{3,2,1,0:T(8,128)(2,1)} %modes.1, bf16[4,4,2,40,40]{4,3,2,1,0:T(8,128)(2,1)} %vectors.1, f32[4,4,40]{2,1,0:T(4,128)} %levels.1, ...), custom_call_target="tpu_custom_call" | custom-call | tf_op jit(solution)/shard_map/widths/pallas_call | solution.py:666
  46.0 1.3 %multiply_bitcast_fusion = (f32[4,120]{1,0:T(4,128)}, f32[4,120]{1,0:T(4,128)}) fusion(f32[2,4,120]{2,1,0:T(4,128)} %widths.1), kind=kLoop, calls=%fused_computation | loop fusion | flops 960 | bytes 7680 | tf_op jit(solution)/shard_map/div | solution.py:751

commit v2 on v1

--- a/solution.py
+++ b/solution.py
@@ -313,10 +313,11 @@
 def ring_kernel(
     pairs, kpoints, qpoints, electron_cells, phonon_cells, modes, vectors,
     levels, filled, energy_k, occupation_k, omega, bose, edge_ref, x_hbm, out_ref,
-    wq, wk, half, ring, parts, recv, relay, sums, table, lifted, rows_ref, turned,
-    emission, absorption, totals, got_e, got_p,
-    ring_sem, relay_send, relay_recv, plane_send, plane_recv, raw_send, raw_recv,
-    sum_send, sum_recv, send_e, recv_e, send_p, recv_p,
+    wq, wk, half, ring, parts, from_plane, from_line, outer_in, inner_in, table, lifted,
+    rows_ref, turned, emission, absorption, vectors_all, levels_all, filled_all, scalars_own,
+    scalars_all, totals_e, totals_p, got_e, got_p,
+    ring_sem, input_sem, input_send, input_recv, outer_send, outer_recv, inner_send, inner_recv,
+    plane_send, plane_recv, line_send, line_recv, send_e, recv_e, send_p, recv_p,
 ):
     step = pl.program_id(0)
     steps = pl.num_programs(0)
@@ -330,14 +331,20 @@
     slots, unit = ring.shape[0], ring.shape[2]
     chunks = cells // unit
     tiles = parts.shape[0]
-    halves = parts.shape[3]
-    mine = 2 * halves
     q_local, k_local = vectors.shape[0], vectors.shape[1]
-    rows = 2 * k_local
+    k_side = 2 * k_local
+    rows = 2 * k_side
+    chips = bands // 2
     bands_n = vectors.shape[3]
     bands_own = bands_n // bands
-    up, down = lax.rem(my_ka + 1, kas), lax.rem(my_ka + kas - 1, kas)
-    across = lax.rem(my_ka + 2, kas)
+    side = my_ka // 2
+    far = 1 - side
+    owner = side * (kas - 1)
+    outer = my_ka == owner
+    inner = jnp.logical_not(outer)
+    partner = side * kas // 2 + lax.rem(my_ka + 1, 2)
+    middle = kas - 1 - my_ka
+    place = lax.rem(my_ka, 2)
     barrier = pltpu.get_barrier_semaphore()
     overlaps = []
     for tile in range(tiles):
@@ -366,18 +373,13 @@
         return half[index * cells : (index + 1) * cells, :].astype(jnp.bfloat16)
 
     def contract(order):
-        for group in range(q_total // 2):
-            products = []
-            for member in range(2):
-                q = group * 2 + member
-                right = jnp.concatenate([strip(q), strip(q_total + q)], axis=0)
-                products.append(jnp.dot(wk[...], right, preferred_element_type=jnp.float32))
-            m = group % mine
-            for ka in range(kas):
-                block = slice(ka * rows, (ka + 1) * rows)
-                parts[order, ka, m // halves, m % halves, group // mine] = jnp.concatenate(
-                    [products[0][block], products[1][block]], axis=0
-                ).astype(jnp.bfloat16)
+        for q in range(q_total):
+            right = jnp.concatenate([strip(q), strip(q_total + q)], axis=0)
+            product = jnp.dot(wk[...], right, preferred_element_type=jnp.float32)
+            for way in range(2):
+                parts[order, way, q // q_local, q % q_local] = product[
+                    way * rows : (way + 1) * rows
+                ].astype(jnp.bfloat16)
 
     def put(source, target, send_sem, recv_sem, to_pb, to_ka):
         pltpu.make_async_remote_copy(
@@ -388,43 +390,60 @@
     def settle(window, sem):
         pltpu.make_async_copy(window, window, sem).wait()
 
+    def chunk_of(index):
+        return pl.ds(2 * lax.rem(my_pb // 2 + 1 + index, chips), 2)
+
     def send(order):
-        put(parts.at[order, across, 0], relay.at[order, 0], relay_send.at[0, order],
-            relay_recv.at[0, order], my_pb, up)
-        put(parts.at[order, across, 1], relay.at[order, 1], relay_send.at[1, order],
-            relay_recv.at[1, order], my_pb, down)
-
-        def raw(index, carry):
-            to = lax.rem(my_pb + index, bands)
-            put(parts.at[order, up, 1, :, to], recv.at[order, 1, 1, :, my_pb],
-                raw_send.at[0, order], raw_recv.at[0, order], to, up)
-            put(parts.at[order, down, 0, :, to], recv.at[order, 2, 0, :, my_pb],
-                raw_send.at[1, order], raw_recv.at[1, order], to, down)
+        @pl.when(outer)
+        def _():
+            def chunk(index, carry):
+                span = chunk_of(index)
+                put(parts.at[order, far, span], outer_in.at[order, span],
+                    outer_send.at[order, index], outer_recv.at[order, index], my_pb, partner)
+                return carry
+
+            lax.fori_loop(0, chips, chunk, 0)
+
+            def plane(index, carry):
+                to = lax.rem(my_pb + index, bands)
+                put(parts.at[order, side, to], from_plane.at[order, my_pb],
+                    plane_send.at[order], plane_recv.at[order], to, my_ka)
+                return carry
+
+            lax.fori_loop(1, bands, plane, 0)
+
+    def added(order, way, span, arrived):
+        own = parts[order, way, span].astype(jnp.float32)
+        parts[order, way, span] = (own + arrived.astype(jnp.float32)).astype(jnp.bfloat16)
+
+    def pass_far(order):
+        def chunk(index, carry):
+            span = chunk_of(index)
+            settle(outer_in.at[order, span], outer_recv.at[order, index])
+            added(order, far, span, outer_in[order, span])
+            put(parts.at[order, far, span], inner_in.at[order, span],
+                inner_send.at[order, index], inner_recv.at[order, index], my_pb, middle)
             return carry
 
-        lax.fori_loop(0, bands, raw, 0)
-
-        def plane(index, carry):
-            to = lax.rem(my_pb + index, bands)
-            put(parts.at[order, my_ka, :, :, to], recv.at[order, 0, :, :, my_pb],
-                plane_send.at[order], plane_recv.at[order], to, my_ka)
+        lax.fori_loop(0, chips, chunk, 0)
+
+    def pass_near(order):
+        def chunk(index, carry):
+            span = chunk_of(index)
+            settle(inner_in.at[order, span], inner_recv.at[order, index])
+            added(order, side, span, inner_in[order, span])
+            for core in range(2):
+                to = 2 * lax.rem(my_pb // 2 + 1 + index, chips) + core
+                put(parts.at[order, side, to], from_line.at[order, my_pb],
+                    line_send.at[order], line_recv.at[order], to, partner)
             return carry
 
-        lax.fori_loop(1, bands, plane, 0)
-
-    def pass_on(order):
-        for way, (target, place) in enumerate(((up, 1), (down, 2))):
-            settle(relay.at[order, way], relay_recv.at[way, order])
-            own = parts[order, target, way].astype(jnp.float32)
-            sums[order, way] = (own + relay[order, way].astype(jnp.float32)).astype(jnp.bfloat16)
-
-            def one(index, carry, way=way, target=target, place=place):
-                to = lax.rem(my_pb + index, bands)
-                put(sums.at[order, way, :, to], recv.at[order, place, way, :, my_pb],
-                    sum_send.at[way, order], sum_recv.at[way, order], to, target)
-                return carry
-
-            lax.fori_loop(0, bands, one, 0)
+        lax.fori_loop(0, chips, chunk, 0)
+
+    inputs = (
+        (vectors, vectors_all), (levels, levels_all), (filled, filled_all),
+        (scalars_own, scalars_all),
+    )
 
     edge_cells = edge_ref.shape[1]
 
@@ -461,44 +480,20 @@
             own = jnp.where(my_ka == ka, cells_all[:, ka * cells : (ka + 1) * cells], own)
         cos, sin = angles(kpoints[...], own)
         blocks = []
-        for ka in range(kas):
-            c = cos[ka * k_local : (ka + 1) * k_local]
-            s = sin[ka * k_local : (ka + 1) * k_local]
+        for way in range(2):
+            c = cos[way * k_side : (way + 1) * k_side]
+            s = sin[way * k_side : (way + 1) * k_side]
             blocks += [jnp.concatenate([c, -s], 1), jnp.concatenate([s, c], 1)]
         wk[...] = jnp.concatenate(blocks, 0).astype(jnp.bfloat16)
+        for k in range(k_local):
+            scalars_own[0, k : k + 1, :] = jnp.full((1, LANES), energy_k[k], jnp.float32)
+            scalars_own[1, k : k + 1, :] = jnp.full((1, LANES), occupation_k[k], jnp.float32)
 
     lax.fori_loop(0, edge_cells // unit, edge, 0)
 
     @pl.when(step == 0)
     def _():
         for q in range(q_local):
-            freq = omega[q : q + 1, :]
-            boson = bose[q : q + 1, :]
-            level_q = jnp.transpose(levels[q])
-            filled_q = jnp.transpose(filled[q])
-            for k in range(k_local):
-                f = filled_q[:, k : k + 1]
-                offset = energy_k[k] - level_q[:, k : k + 1]
-                absorb = gaussian(offset + freq)
-                emit = gaussian(offset - freq)
-                emission[q, k] = (boson + f) * absorb + (boson + 1.0 - f) * emit
-                absorption[q, k] = (occupation_k[k] - f) * absorb
-                for part in range(2):
-                    rows_ref[part, :, :bands_n] = vectors[q, k, part].astype(jnp.float32)
-                real, imag = (
-                    jnp.concatenate(
-                        [
-                            rows_ref[part, pl.ds(n, bands, stride=bands_own), :]
-                            for n in range(bands_own)
-                        ],
-                        axis=0,
-                    )[:, :bands_n]
-                    for part in range(2)
-                )
-                both = jnp.concatenate(
-                    [jnp.concatenate([real, -imag], 1), jnp.concatenate([imag, real], 1)], 0
-                )
-                turned[q, k] = jnp.transpose(both).astype(jnp.bfloat16)
             for part in range(2):
                 mode = modes[q, part].astype(jnp.float32)
                 for index, (tile, n, row, start, count) in enumerate(overlaps):
@@ -513,83 +508,84 @@
                         jnp.bfloat16
                     )
 
-    @pl.when(step == steps - 1)
-    def _():
-        contract(0)
-        pl.semaphore_wait(barrier, devices - 1)
-        send(0)
-
-        def one_tile(tile, carry):
-            def one_chunk(chunk, inner_carry):
-                index = tile * chunks + chunk
-                slot = lax.rem(index, slots)
-                fetch(index, slot).wait()
-                for inner in range(unit):
-                    project(ring[slot, 0, inner], ring[slot, 1, inner], chunk * unit + inner)
-
-                @pl.when(index + slots < (tiles - 1) * chunks)
-                def _():
-                    fetch(index + slots, slot).start()
-
-                return inner_carry
-
-            lax.fori_loop(0, chunks, one_chunk, 0)
-            contract(tile + 1)
-            send(tile + 1)
-            pass_on(tile)
-            return carry
-
-        lax.fori_loop(0, tiles - 1, one_tile, 0)
+    def prepare(block, q):
+        freq = omega[pl.ds(q, 1), :]
+        boson = bose[pl.ds(q, 1), :]
+        level_q = jnp.transpose(levels_all[block, q])
+        filled_q = jnp.transpose(filled_all[block, q])
+        for k in range(k_local):
+            f = filled_q[:, k : k + 1]
+            offset = scalars_all[block, 0, k : k + 1, :1] - level_q[:, k : k + 1]
+            absorb = gaussian(offset + freq)
+            emit = gaussian(offset - freq)
+            spot = block * k_local + k
+            emission[q, spot] = (boson + f) * absorb + (boson + 1.0 - f) * emit
+            absorption[q, spot] = (scalars_all[block, 1, k : k + 1, :1] - f) * absorb
+            for part in range(2):
+                rows_ref[k, part, :, :bands_n] = vectors_all[block, q, k, part].astype(jnp.float32)
+            real, imag = (
+                jnp.concatenate(
+                    [
+                        rows_ref[k, part, pl.ds(n, bands, stride=bands_own), :]
+                        for n in range(bands_own)
+                    ],
+                    axis=0,
+                )[:, :bands_n]
+                for part in range(2)
+            )
+            both = jnp.concatenate(
+                [jnp.concatenate([real, -imag], 1), jnp.concatenate([imag, real], 1)], 0
+            )
+            turned[q, spot] = jnp.transpose(both).astype(jnp.bfloat16)
+
+    def finish():
+        for number, (_, target) in enumerate(inputs):
+            settle(target.at[0], input_recv.at[number])
+        for number, (source, target) in enumerate(inputs):
+            pltpu.make_async_copy(source, target.at[place], input_sem.at[number]).wait()
+        for block in range(2):
+            for q in range(q_local):
+                prepare(block, q)
         for order in range(tiles):
-            recv[order, 0, :, :, my_pb] = parts[order, my_ka, :, :, my_pb]
-        pass_on(tiles - 1)
+            from_plane[order, my_pb] = parts[order, side, my_pb]
         lane = lax.broadcasted_iota(jnp.int32, (1, LANES), 1)
         started = set()
         for order in range(tiles):
             tile = tiles - 1 if order == 0 else order - 1
-            settle(recv.at[order, 0, :, :, pl.ds(1, bands - 1)], plane_recv.at[order])
-            for way in range(2):
-                settle(recv.at[order, 1 + way, 1 - way], raw_recv.at[way, order])
-            for way in range(2):
-                settle(recv.at[order, 1 + way, way], sum_recv.at[way, order])
-            for m in range(mine):
-                spot = (m // halves, m % halves)
-                total = [
-                    recv[order, 0, *spot, band].astype(jnp.float32)
-                    + recv[order, 1, *spot, band].astype(jnp.float32)
-                    + recv[order, 2, *spot, band].astype(jnp.float32)
-                    for band in range(bands)
-                ]
-                for member in range(2):
-                    q = 2 * m + member
-                    left = jnp.concatenate(
-                        [one[member * rows : (member + 1) * rows] for one in total], axis=0
-                    )
-                    if pairs < (tile + 1) * LANES:
-                        left = jnp.where(lane < pairs - tile * LANES, left, 0.0)
-                    left = left.astype(jnp.bfloat16)
-                    for index, (other, n, _, _, _) in enumerate(overlaps):
-                        if other != tile:
-                            continue
-                        product = jnp.dot(
-                            left, table[q, index], preferred_element_type=jnp.float32
-                        )
-                        for side in range(2):
-                            value = product[:, side * LANES : (side + 1) * LANES]
-                            if (q, n) in started:
-                                value = value + lifted[q, n, side]
-                            lifted[q, n, side] = value
-                        started.add((q, n))
-        electron = [None] * k_local
+            settle(from_plane.at[order, pl.ds(1, bands - 1)], plane_recv.at[order])
+            settle(from_line.at[order], line_recv.at[order])
+            for q in range(q_local):
+                left = jnp.concatenate(
+                    [
+                        from_plane[order, band, q].astype(jnp.float32)
+                        + from_line[order, band, q].astype(jnp.float32)
+                        for band in range(bands)
+                    ],
+                    axis=0,
+                )
+                if pairs < (tile + 1) * LANES:
+                    left = jnp.where(lane < pairs - tile * LANES, left, 0.0)
+                left = left.astype(jnp.bfloat16)
+                for index, (other, n, _, _, _) in enumerate(overlaps):
+                    if other != tile:
+                        continue
+                    product = jnp.dot(left, table[q, index], preferred_element_type=jnp.float32)
+                    for half_of in range(2):
+                        value = product[:, half_of * LANES : (half_of + 1) * LANES]
+                        if (q, n) in started:
+                            value = value + lifted[q, n, half_of]
+                        lifted[q, n, half_of] = value
+                    started.add((q, n))
+        electron = [None] * k_side
         for q in range(q_local):
             phonon = None
-            for k in range(k_local):
+            for k in range(k_side):
                 real, imag = [], []
                 for n in range(bands_own):
                     rr, ri, ir, ii = (
-                        lifted[q, n, side, pl.ds(part * k_local + k, bands, stride=rows), :]
+                        lifted[q, n, half_of, pl.ds(part * k_side + k, bands, stride=rows), :]
                         for part in range(2)
-                        for side in range(2)
+                        for half_of in range(2)
                     )
                     real.append(rr - ii)
                     imag.append(ri + ir)
@@ -602,40 +598,111 @@
                 p_term = weight * absorption[q, k]
                 electron[k] = e_term if q == 0 else electron[k] + e_term
                 phonon = p_term if k == 0 else phonon + p_term
-            totals[1, q : q + 1, :] = jnp.sum(phonon, axis=0, keepdims=True)
-        for k in range(k_local):
-            totals[0, k : k + 1, :] = jnp.sum(electron[k], axis=0, keepdims=True)
+            totals_p[q : q + 1, :] = jnp.sum(phonon, axis=0, keepdims=True)
+        for k in range(k_side):
+            totals_e[k // k_local, k % k_local : k % k_local + 1, :] = jnp.sum(
+                electron[k], axis=0, keepdims=True
+            )
         copies = []
+        for shift in range(1, kas):
+            copies.append(pltpu.make_async_remote_copy(
+                totals_p, got_p.at[side], send_p.at[shift - 1], recv_p.at[side],
+                device_id={"pb": my_pb, "ka": lax.rem(my_ka + shift, kas)}, device_id_type=MESH,
+            ))
+        for shift in range(bands):
+            copies.append(pltpu.make_async_remote_copy(
+                totals_e.at[1 - place], got_e.at[my_pb], send_e.at[0, shift], recv_e.at[my_pb],
+                device_id={"pb": lax.rem(my_pb + shift, bands), "ka": partner},
+                device_id_type=MESH,
+            ))
         for shift in range(1, bands):
             copies.append(pltpu.make_async_remote_copy(
-                totals.at[0], got_e.at[my_pb], send_e.at[shift - 1], recv_e.at[shift - 1],
+                totals_e.at[place], got_e.at[my_pb], send_e.at[1, shift], recv_e.at[my_pb],
                 device_id={"pb": lax.rem(my_pb + shift, bands), "ka": my_ka}, device_id_type=MESH,
-            ))
-        for shift in range(1, kas):
-            copies.append(pltpu.make_async_remote_copy(
-                totals.at[1], got_p.at[my_ka], send_p.at[shift - 1], recv_p.at[shift - 1],
-                device_id={"pb": my_pb, "ka": lax.rem(my_ka + shift, kas)}, device_id_type=MESH,
             ))
         for copy in copies:
             copy.start()
-        got_e[my_pb] = totals[0]
-        got_p[my_ka] = totals[1]
+        got_e[my_pb] = totals_e[place]
+        got_p[side] = totals_p[...]
         for order in range(tiles):
-            settle(recv.at[order, 0, :, :, pl.ds(1, bands - 1)], plane_send.at[order])
-            for way in range(2):
-                settle(relay.at[order, way], relay_send.at[way, order])
-                settle(recv.at[order, 1 + way, 1 - way], raw_send.at[way, order])
-                settle(recv.at[order, 1 + way, way], sum_send.at[way, order])
+            settle(from_plane.at[order, pl.ds(1, bands - 1)], plane_send.at[order])
+            for index in range(chips):
+                settle(outer_in.at[order, pl.ds(0, 2)], outer_send.at[order, index])
         for copy in copies:
-            copy.wait()
-        total = got_e[0]
-        for other in range(1, bands):
-            total = total + got_e[other]
+            copy.wait_send()
+        settle(got_p.at[far], recv_p.at[far])
+
+    def relay():
+        pass_near(tiles - 2)
+        pass_far(tiles - 1)
+        pass_near(tiles - 1)
+        for number, (source, _) in enumerate(inputs):
+            settle(source, input_send.at[number])
+        for order in range(tiles):
+            settle(from_line.at[order], line_send.at[order])
+            for index in range(chips):
+                settle(inner_in.at[order, pl.ds(0, 2)], inner_send.at[order, index])
+        for way in range(2):
+            settle(got_p.at[way], recv_p.at[way])
+        settle(got_e.at[my_pb], recv_e.at[my_pb])
+
+    @pl.when(step == steps - 1)
+    def _():
+        pl.semaphore_wait(barrier, devices - 1)
+
+        @pl.when(outer)
+        def _():
+            for number, (source, target) in enumerate(inputs):
+                pltpu.make_async_copy(source, target.at[place], input_sem.at[number]).start()
+
+        @pl.when(inner)
+        def _():
+            for number, (source, target) in enumerate(inputs):
+                put(source, target.at[place], input_send.at[number], input_recv.at[number],
+                    my_pb, partner)
+
+        contract(0)
+        send(0)
+
+        def one_tile(tile, carry):
+            def one_chunk(chunk, inner_carry):
+                index = tile * chunks + chunk
+                slot = lax.rem(index, slots)
+                fetch(index, slot).wait()
+                for inside in range(unit):
+                    project(ring[slot, 0, inside], ring[slot, 1, inside], chunk * unit + inside)
+
+                @pl.when(index + slots < (tiles - 1) * chunks)
+                def _():
+                    fetch(index + slots, slot).start()
+
+                return inner_carry
+
+            lax.fori_loop(0, chunks, one_chunk, 0)
+            contract(tile + 1)
+            send(tile + 1)
+
+            @pl.when(inner)
+            def _():
+                pass_far(tile)
+
+            @pl.when(inner & (tile >= 1))
+            def _():
+                pass_near(tile - 1)
+
+            return carry
+
+        lax.fori_loop(0, tiles - 1, one_tile, 0)
+        pl.when(inner)(relay)
+        pl.when(outer)(finish)
+        total = None
+        for shift in range(1, bands):
+            other = lax.rem(my_pb + shift, bands)
+            settle(got_e.at[other], recv_e.at[other])
+        for other in range(bands):
+            total = got_e[other] if other == 0 else total + got_e[other]
         out_ref[0] = total
-        total = got_p[0]
-        for other in range(1, kas):
-            total = total + got_p[other]
-        out_ref[1] = total
+        out_ref[1] = got_p[0] + got_p[1]
 
 
 def everything(
@@ -651,8 +718,9 @@
     q_local, k_local = band_vectors.shape[0], band_vectors.shape[1]
     bands_n = band_vectors.shape[3]
     columns = 2 * qpoints.shape[1]
-    halves = q_local // 4
-    rows = 4 * k_local
+    k_side = 2 * k_local
+    rows = 2 * k_side
+    chips = bands // 2
     bands_own = bands_n // bands
     overlaps = sum(
         max(t * LANES, n * MODES) < min((t + 1) * LANES, (n + 1) * MODES)
@@ -680,32 +748,42 @@
             pltpu.VMEM((2 * k_local * kas, 2 * cells), bf16),
             pltpu.VMEM((columns * cells, LANES), f32),
             pltpu.VMEM((slots, parts_count, unit, phonons, LANES), bf16),
-            pltpu.VMEM((tiles, kas, 2, halves, bands, rows, LANES), bf16),
-            pltpu.VMEM((tiles, 3, 2, halves, bands, rows, LANES), bf16),
-            pltpu.VMEM((tiles, 2, halves, bands, rows, LANES), bf16),
-            pltpu.VMEM((tiles, 2, halves, bands, rows, LANES), bf16),
+            pltpu.VMEM((tiles, 2, bands, q_local, rows, LANES), bf16),
+            pltpu.VMEM((tiles, bands, q_local, rows, LANES), bf16),
+            pltpu.VMEM((tiles, bands, q_local, rows, LANES), bf16),
+            pltpu.VMEM((tiles, bands, q_local, rows, LANES), bf16),
+            pltpu.VMEM((tiles, bands, q_local, rows, LANES), bf16),
             pltpu.VMEM((q_local, overlaps, LANES, 2 * LANES), bf16),
-            pltpu.VMEM((q_local, bands_own, 2, bands * 2 * k_local, LANES), f32),
-            pltpu.VMEM((2, bands_n, LANES), f32),
-            pltpu.VMEM((q_local, k_local, 2 * bands_n, 2 * bands_n), bf16),
-            pltpu.VMEM((q_local, k_local, bands_n, MODES), f32),
-            pltpu.VMEM((q_local, k_local, bands_n, MODES), f32),
+            pltpu.VMEM((q_local, bands_own, 2, bands * rows, LANES), f32),
+            pltpu.VMEM((k_local, 2, bands_n, LANES), f32),
+            pltpu.VMEM((q_local, k_side, 2 * bands_n, 2 * bands_n), bf16),
+            pltpu.VMEM((q_local, k_side, bands_n, MODES), f32),
+            pltpu.VMEM((q_local, k_side, bands_n, MODES), f32),
+            pltpu.VMEM((2, *band_vectors.shape), bf16),
+            pltpu.VMEM((2, *energies_kq.shape), f32),
+            pltpu.VMEM((2, *occupations_kq.shape), f32),
+            pltpu.VMEM((2, k_local, LANES), f32),
+            pltpu.VMEM((2, 2, k_local, LANES), f32),
             pltpu.VMEM((2, k_local, MODES), f32),
+            pltpu.VMEM((q_local, MODES), f32),
             pltpu.VMEM((bands, k_local, MODES), f32),
-            pltpu.VMEM((kas, k_local, MODES), f32),
+            pltpu.VMEM((2, q_local, MODES), f32),
             dma((slots,)),
-            dma((2, tiles)),
-            dma((2, tiles)),
+            dma((4,)),
+            dma((4,)),
+            dma((4,)),
+            dma((tiles, chips)),
+            dma((tiles, chips)),
+            dma((tiles, chips)),
+            dma((tiles, chips)),
             dma((tiles,)),
             dma((tiles,)),
-            dma((2, tiles)),
-            dma((2, tiles)),
-            dma((2, tiles)),
-            dma((2, tiles)),
-            dma((bands - 1,)),
-            dma((bands - 1,)),
+            dma((tiles,)),
+            dma((tiles,)),
+            dma((2, bands)),
+            dma((bands,)),
             dma((kas - 1,)),
-            dma((kas - 1,)),
+            dma((2,)),
         ],
         compiler_params=pltpu.CompilerParams(
             collective_id=2,
@@ -742,7 +820,7 @@
     q_total = q_local * bands
     k_total = k_local * kas
     whole_bands = coupling.shape[2] % MODES == 0 and coupling.shape[2] > LANES
-    even = q_local % 4 == 0 and cells_local % 16 == 0
+    even = bands % 2 == 0 and cells_local % 16 == 0
     if kas == 4 and whole_bands and even and k_local == q_local:
         sums = everything(
             coupling, kpoints, qpoints, electron_cells, phonon_cells, phonon_modes, band_vectors,

time: 47.5 us -> 49.2 us (1.036)
  Pallas kernels: 45.4 us -> 47.1 us
    pallas_call x1, Pallas kernels: 45.4 us -> 47.1 us  [everything(): pl.pallas_call(functools.partial(ring_kernel, pairs), grid=(2,), in_specs...]
where the time goes in v2:
time: 49.2 us; the launch traced here: 49 us
  Pallas kernels  47.1 us (96%)
  other arithmetic  1.26 us (3%)
  between operations  0.64 us (1%)
    pallas_call x1, Pallas kernels, everything(): pl.pallas_call(functools.partial(ring_kernel, pairs), grid=(2,), in_specs...  47.1 us
    div x1, other arithmetic, on_device(): return (sums[0] / (q_total * NB), sums[1] / (k_total * NB))  1.26 us

profile of v2, /device:TPU:0, one launch (start us, length us, event | category | flops | bytes accessed | tf_op | source)
XLA Modules:
  0.0 49.0 jit_solution(17128144769877198358)
XLA Ops:
  0.6 47.1 %widths.1 = f32[2,4,120]{2,1,0:T(4,128)} custom-call(s32[3,16]{1,0:T(4,128)} %kpoints.1, s32[3,32]{1,0:T(4,128)} %qpoints.1, s32[3,320]{1,0:T(4,128)} %electron_cells.1, s32[3,320]{1,0:T(4,128)} %phonon_cells.1, bf16[4,2,120,120]{3,2,1,0:T(8,128)(2,1)} %modes.1, bf16[4,4,2,40,40]{4,3,2,1,0:T(8,128)(2,1)} %vectors.1, f32[4,4,40]{2,1,0:T(4,128)} %levels.1, ...), custom_call_target="tpu_custom_call" | custom-call | tf_op jit(solution)/shard_map/widths/pallas_call | solution.py:734
  47.7 1.3 %multiply_bitcast_fusion = (f32[4,120]{1,0:T(4,128)}, f32[4,120]{1,0:T(4,128)}) fusion(f32[2,4,120]{2,1,0:T(4,128)} %widths.1), kind=kLoop, calls=%fused_computation | loop fusion | flops 960 | bytes 7680 | tf_op jit(solution)/shard_map/div | solution.py:829

commit v3 on v1

--- a/solution.py
+++ b/solution.py
@@ -326,7 +326,8 @@
     me = my_pb * kas + my_ka
     columns = wq.shape[0]
     q_total = columns // 2
-    cells = half.shape[0] // columns
+    pitch = half.shape[0] // columns
+    cells = wk.shape[1] // 2
     slots, unit = ring.shape[0], ring.shape[2]
     chunks = cells // unit
     tiles = parts.shape[0]
@@ -360,10 +361,10 @@
     def project(real, imag, row):
         right = jnp.concatenate([real, imag], axis=0)
         product = jnp.dot(wq[...], right, preferred_element_type=jnp.float32)
-        half[pl.ds(row, columns, stride=cells), :] = product
+        half[pl.ds(row, columns, stride=pitch), :] = product
 
     def strip(index):
-        return half[index * cells : (index + 1) * cells, :].astype(jnp.bfloat16)
+        return half[index * pitch : index * pitch + cells, :].astype(jnp.bfloat16)
 
     def contract(order):
         for group in range(q_total // 2):
@@ -536,12 +537,17 @@
             lax.fori_loop(0, chunks, one_chunk, 0)
             contract(tile + 1)
             send(tile + 1)
-            pass_on(tile)
+
+            @pl.when(tile >= 1)
+            def _():
+                pass_on(tile - 1)
+
             return carry
 
         lax.fori_loop(0, tiles - 1, one_tile, 0)
         for order in range(tiles):
             recv[order, 0, :, :, my_pb] = parts[order, my_ka, :, :, my_pb]
+        pass_on(tiles - 2)
         pass_on(tiles - 1)
         lane = lax.broadcasted_iota(jnp.int32, (1, LANES), 1)
         started = set()
@@ -647,6 +653,7 @@
     moved = jnp.transpose(coupling, (0, 1, 3, 2))
     tiles = -(-pairs // LANES)
     unit = cells // 4
+    pitch = 8 * (-(-cells // 8) | 1)
     slots = 8
     q_local, k_local = band_vectors.shape[0], band_vectors.shape[1]
     bands_n = band_vectors.shape[3]
@@ -678,7 +685,7 @@
         scratch_shapes=[
             pltpu.VMEM((columns, 2 * phonons), bf16),
             pltpu.VMEM((2 * k_local * kas, 2 * cells), bf16),
-            pltpu.VMEM((columns * cells, LANES), f32),
+            pltpu.VMEM((columns * pitch, LANES), f32),
             pltpu.VMEM((slots, parts_count, unit, phonons, LANES), bf16),
             pltpu.VMEM((tiles, kas, 2, halves, bands, rows, LANES), bf16),
             pltpu.VMEM((tiles, 3, 2, halves, bands, rows, LANES), bf16),

time: 47.5 us -> 46 us (0.968)
  Pallas kernels: 45.4 us -> 43.9 us
    pallas_call x1, Pallas kernels: 45.4 us -> 43.9 us  [everything(): pl.pallas_call(functools.partial(ring_kernel, pairs), grid=(2,), in_specs...]
where the time goes in v3:
time: 46 us; the launch traced here: 45.8 us
  Pallas kernels  43.9 us (95%)
  other arithmetic  1.26 us (3%)
  between operations  0.64 us (1%)
    pallas_call x1, Pallas kernels, everything(): pl.pallas_call(functools.partial(ring_kernel, pairs), grid=(2,), in_specs...  43.9 us
    div x1, other arithmetic, on_device(): return (sums[0] / (q_total * NB), sums[1] / (k_total * NB))  1.26 us

profile of v3, /device:TPU:0, one launch (start us, length us, event | category | flops | bytes accessed | tf_op | source)
XLA Modules:
  0.0 45.8 jit_solution(6017444353718497195)
XLA Ops:
  0.6 43.9 %widths.1 = f32[2,4,120]{2,1,0:T(4,128)} custom-call(s32[3,16]{1,0:T(4,128)} %kpoints.1, s32[3,32]{1,0:T(4,128)} %qpoints.1, s32[3,320]{1,0:T(4,128)} %electron_cells.1, s32[3,320]{1,0:T(4,128)} %phonon_cells.1, bf16[4,2,120,120]{3,2,1,0:T(8,128)(2,1)} %modes.1, bf16[4,4,2,40,40]{4,3,2,1,0:T(8,128)(2,1)} %vectors.1, f32[4,4,40]{2,1,0:T(4,128)} %levels.1, ...), custom_call_target="tpu_custom_call" | custom-call | tf_op jit(solution)/shard_map/widths/pallas_call | solution.py:673
  44.5 1.3 %multiply_bitcast_fusion = (f32[4,120]{1,0:T(4,128)}, f32[4,120]{1,0:T(4,128)}) fusion(f32[2,4,120]{2,1,0:T(4,128)} %widths.1), kind=kLoop, calls=%fused_computation | loop fusion | flops 960 | bytes 7680 | tf_op jit(solution)/shard_map/div | solution.py:758

commit v4 on v3

--- a/solution.py
+++ b/solution.py
@@ -368,16 +368,19 @@
 
     def contract(order):
         for group in range(q_total // 2):
-            products = []
-            for member in range(2):
-                q = group * 2 + member
-                right = jnp.concatenate([strip(q), strip(q_total + q)], axis=0)
-                products.append(jnp.dot(wk[...], right, preferred_element_type=jnp.float32))
+            right = jnp.concatenate(
+                [
+                    jnp.concatenate([strip(q), strip(q_total + q)], axis=0)
+                    for q in (group * 2, group * 2 + 1)
+                ],
+                axis=1,
+            )
+            product = jnp.dot(wk[...], right, preferred_element_type=jnp.float32)
             m = group % mine
             for ka in range(kas):
                 block = slice(ka * rows, (ka + 1) * rows)
                 parts[order, ka, m // halves, m % halves, group // mine] = jnp.concatenate(
-                    [products[0][block], products[1][block]], axis=0
+                    [product[block, :LANES], product[block, LANES:]], axis=0
                 ).astype(jnp.bfloat16)
 
     def put(source, target, send_sem, recv_sem, to_pb, to_ka):
@@ -470,8 +473,7 @@
 
     lax.fori_loop(0, edge_cells // unit, edge, 0)
 
-    @pl.when(step == 0)
-    def _():
+    def prepare():
         for q in range(q_local):
             freq = omega[q : q + 1, :]
             boson = bose[q : q + 1, :]
@@ -549,6 +551,7 @@
             recv[order, 0, :, :, my_pb] = parts[order, my_ka, :, :, my_pb]
         pass_on(tiles - 2)
         pass_on(tiles - 1)
+        prepare()
         lane = lax.broadcasted_iota(jnp.int32, (1, LANES), 1)
         started = set()
         for order in range(tiles):
@@ -652,9 +655,9 @@
     parts_count, cells, pairs, phonons = coupling.shape
     moved = jnp.transpose(coupling, (0, 1, 3, 2))
     tiles = -(-pairs // LANES)
-    unit = cells // 4
+    unit = cells // 2
     pitch = 8 * (-(-cells // 8) | 1)
-    slots = 8
+    slots = 4
     q_local, k_local = band_vectors.shape[0], band_vectors.shape[1]
     bands_n = band_vectors.shape[3]
     columns = 2 * qpoints.shape[1]

time: 46 us -> 43.7 us (0.950)
  Pallas kernels: 43.9 us -> 41.7 us
    pallas_call x1, Pallas kernels: 43.9 us -> 41.7 us  [everything(): pl.pallas_call(functools.partial(ring_kernel, pairs), grid=(2,), in_specs...]
where the time goes in v4:
time: 43.7 us; the launch traced here: 43.6 us
  Pallas kernels  41.7 us (95%)
  other arithmetic  1.26 us (3%)
  between operations  0.64 us (1%)
    pallas_call x1, Pallas kernels, everything(): pl.pallas_call(functools.partial(ring_kernel, pairs), grid=(2,), in_specs...  41.7 us
    div x1, other arithmetic, on_device(): return (sums[0] / (q_total * NB), sums[1] / (k_total * NB))  1.26 us

profile of v4, /device:TPU:0, one launch (start us, length us, event | category | flops | bytes accessed | tf_op | source)
XLA Modules:
  0.0 43.6 jit_solution(3881900581304171984)
XLA Ops:
  0.6 41.7 %widths.1 = f32[2,4,120]{2,1,0:T(4,128)} custom-call(s32[3,16]{1,0:T(4,128)} %kpoints.1, s32[3,32]{1,0:T(4,128)} %qpoints.1, s32[3,320]{1,0:T(4,128)} %electron_cells.1, s32[3,320]{1,0:T(4,128)} %phonon_cells.1, bf16[4,2,120,120]{3,2,1,0:T(8,128)(2,1)} %modes.1, bf16[4,4,2,40,40]{4,3,2,1,0:T(8,128)(2,1)} %vectors.1, f32[4,4,40]{2,1,0:T(4,128)} %levels.1, ...), custom_call_target="tpu_custom_call" | custom-call | tf_op jit(solution)/shard_map/widths/pallas_call | solution.py:676
  42.3 1.3 %multiply_bitcast_fusion = (f32[4,120]{1,0:T(4,128)}, f32[4,120]{1,0:T(4,128)}) fusion(f32[2,4,120]{2,1,0:T(4,128)} %widths.1), kind=kLoop, calls=%fused_computation | loop fusion | flops 960 | bytes 7680 | tf_op jit(solution)/shard_map/div | solution.py:761

commit v5 on v4

--- a/solution.py
+++ b/solution.py
@@ -340,6 +340,10 @@
     up, down = lax.rem(my_ka + 1, kas), lax.rem(my_ka + kas - 1, kas)
     across = lax.rem(my_ka + 2, kas)
     barrier = pltpu.get_barrier_semaphore()
+    valid = pairs - (tiles - 1) * LANES
+    spare = LANES - valid
+    packed = q_local == 4 and valid <= 3 * spare
+    lane = lax.broadcasted_iota(jnp.int32, (1, LANES), 1)
     overlaps = []
     for tile in range(tiles):
         for n in range(bands_own):
@@ -366,7 +370,8 @@
     def strip(index):
         return half[index * pitch : index * pitch + cells, :].astype(jnp.bfloat16)
 
-    def contract(order):
+    def contract(order, pack=False):
+        waiting = []
         for group in range(q_total // 2):
             right = jnp.concatenate(
                 [
@@ -376,12 +381,20 @@
                 axis=1,
             )
             product = jnp.dot(wk[...], right, preferred_element_type=jnp.float32)
-            m = group % mine
-            for ka in range(kas):
-                block = slice(ka * rows, (ka + 1) * rows)
-                parts[order, ka, m // halves, m % halves, group // mine] = jnp.concatenate(
-                    [product[block, :LANES], product[block, LANES:]], axis=0
-                ).astype(jnp.bfloat16)
+            waiting += [product[:, :LANES], product[:, LANES:]]
+            if len(waiting) < q_local:
+                continue
+            if pack:
+                for host in range(3):
+                    moved = pltpu.roll(waiting[3], (valid - host * spare) % LANES, 1)
+                    waiting[host] = jnp.where(lane < valid, waiting[host], moved)
+            for q in range(q_local):
+                m = q // 2
+                for ka in range(kas):
+                    parts[order, ka, m // halves, m % halves, group // mine, q % 2] = waiting[q][
+                        ka * rows : (ka + 1) * rows
+                    ].astype(jnp.bfloat16)
+            waiting = []
 
     def put(source, target, send_sem, recv_sem, to_pb, to_ka):
         pltpu.make_async_remote_copy(
@@ -392,18 +405,23 @@
     def settle(window, sem):
         pltpu.make_async_copy(window, window, sem).wait()
 
-    def send(order):
-        put(parts.at[order, across, 0], relay.at[order, 0], relay_send.at[0, order],
-            relay_recv.at[0, order], my_pb, up)
-        put(parts.at[order, across, 1], relay.at[order, 1], relay_send.at[1, order],
-            relay_recv.at[1, order], my_pb, down)
+    def lot(ref, way, pack):
+        return ref.at[:, :, 0] if pack and way == 1 else ref
+
+    def item(ref, way, to, pack):
+        return ref.at[:, to, 0] if pack and way == 1 else ref.at[:, to]
+
+    def send(order, pack=False):
+        for way, target in enumerate((up, down)):
+            put(lot(parts.at[order, across, way], way, pack), lot(relay.at[order, way], way, pack),
+                relay_send.at[way, order], relay_recv.at[way, order], my_pb, target)
 
         def raw(index, carry):
             to = lax.rem(my_pb + index, bands)
-            put(parts.at[order, up, 1, :, to], recv.at[order, 1, 1, :, my_pb],
-                raw_send.at[0, order], raw_recv.at[0, order], to, up)
-            put(parts.at[order, down, 0, :, to], recv.at[order, 2, 0, :, my_pb],
-                raw_send.at[1, order], raw_recv.at[1, order], to, down)
+            for way, target in enumerate((down, up)):
+                put(item(parts.at[order, target, way], way, to, pack),
+                    item(recv.at[order, 2 - way, way], way, my_pb, pack),
+                    raw_send.at[1 - way, order], raw_recv.at[1 - way, order], to, target)
             return carry
 
         lax.fori_loop(0, bands, raw, 0)
@@ -416,15 +434,18 @@
 
         lax.fori_loop(1, bands, plane, 0)
 
-    def pass_on(order):
+    def pass_on(order, pack=False):
         for way, (target, place) in enumerate(((up, 1), (down, 2))):
-            settle(relay.at[order, way], relay_recv.at[way, order])
-            own = parts[order, target, way].astype(jnp.float32)
-            sums[order, way] = (own + relay[order, way].astype(jnp.float32)).astype(jnp.bfloat16)
+            settle(lot(relay.at[order, way], way, pack), relay_recv.at[way, order])
+            for member in range(1 if pack and way == 1 else 2):
+                own = parts[order, target, way, :, :, member].astype(jnp.float32)
+                arrived = relay[order, way, :, :, member].astype(jnp.float32)
+                sums[order, way, :, :, member] = (own + arrived).astype(jnp.bfloat16)
 
             def one(index, carry, way=way, target=target, place=place):
                 to = lax.rem(my_pb + index, bands)
-                put(sums.at[order, way, :, to], recv.at[order, place, way, :, my_pb],
+                put(item(sums.at[order, way], way, to, pack),
+                    item(recv.at[order, place, way], way, my_pb, pack),
                     sum_send.at[way, order], sum_recv.at[way, order], to, target)
                 return carry
 
@@ -518,12 +539,12 @@
 
     @pl.when(step == steps - 1)
     def _():
-        contract(0)
+        contract(0, packed)
         pl.semaphore_wait(barrier, devices - 1)
-        send(0)
+        send(0, packed)
 
         def one_tile(tile, carry):
-            def one_chunk(chunk, inner_carry):
+            for chunk in range(chunks):
                 index = tile * chunks + chunk
                 slot = lax.rem(index, slots)
                 fetch(index, slot).wait()
@@ -531,49 +552,65 @@
                     project(ring[slot, 0, inner], ring[slot, 1, inner], chunk * unit + inner)
 
                 @pl.when(index + slots < (tiles - 1) * chunks)
-                def _():
+                def _(index=index, slot=slot):
                     fetch(index + slots, slot).start()
 
-                return inner_carry
-
-            lax.fori_loop(0, chunks, one_chunk, 0)
+                if chunk == 0:
+
+                    @pl.when(tile == 1)
+                    def _():
+                        pass_on(0, packed)
+
+                    @pl.when(tile > 1)
+                    def _():
+                        pass_on(tile - 1)
+
             contract(tile + 1)
             send(tile + 1)
 
-            @pl.when(tile >= 1)
-            def _():
-                pass_on(tile - 1)
 
             return carry
 
         lax.fori_loop(0, tiles - 1, one_tile, 0)
         for order in range(tiles):
             recv[order, 0, :, :, my_pb] = parts[order, my_ka, :, :, my_pb]
-        pass_on(tiles - 2)
+        pass_on(tiles - 2, packed and tiles == 2)
         pass_on(tiles - 1)
         prepare()
-        lane = lax.broadcasted_iota(jnp.int32, (1, LANES), 1)
         started = set()
         for order in range(tiles):
             tile = tiles - 1 if order == 0 else order - 1
             settle(recv.at[order, 0, :, :, pl.ds(1, bands - 1)], plane_recv.at[order])
+            pack = packed and order == 0
             for way in range(2):
-                settle(recv.at[order, 1 + way, 1 - way], raw_recv.at[way, order])
+                window = recv.at[order, 1 + way, 1 - way]
+                settle(lot(window, 1 - way, pack), raw_recv.at[way, order])
             for way in range(2):
-                settle(recv.at[order, 1 + way, way], sum_recv.at[way, order])
+                settle(lot(recv.at[order, 1 + way, way], way, pack), sum_recv.at[way, order])
+            lefts = []
+            for q in range(q_local - 1 if pack else q_local):
+                m = q // 2
+                spot = (m // halves, m % halves)
+                lefts.append(jnp.concatenate(
+                    [
+                        recv[order, 0, *spot, band, q % 2].astype(jnp.float32)
+                        + recv[order, 1, *spot, band, q % 2].astype(jnp.float32)
+                        + recv[order, 2, *spot, band, q % 2].astype(jnp.float32)
+                        for band in range(bands)
+                    ],
+                    axis=0,
+                ))
+            if pack:
+                back = [
+                    pltpu.roll(lefts[host], (host * spare - valid) % LANES, 1) for host in range(3)
+                ]
+                lefts.append(
+                    jnp.where(lane < spare, back[0], jnp.where(lane < 2 * spare, back[1], back[2]))
+                )
             for m in range(mine):
-                spot = (m // halves, m % halves)
-                total = [
-                    recv[order, 0, *spot, band].astype(jnp.float32)
-                    + recv[order, 1, *spot, band].astype(jnp.float32)
-                    + recv[order, 2, *spot, band].astype(jnp.float32)
-                    for band in range(bands)
-                ]
                 for member in range(2):
                     q = 2 * m + member
-                    left = jnp.concatenate(
-                        [one[member * rows : (member + 1) * rows] for one in total], axis=0
-                    )
+                    left = lefts[q]
                     if pairs < (tile + 1) * LANES:
                         left = jnp.where(lane < pairs - tile * LANES, left, 0.0)
                     left = left.astype(jnp.bfloat16)
@@ -631,10 +668,12 @@
         got_p[my_ka] = totals[1]
         for order in range(tiles):
             settle(recv.at[order, 0, :, :, pl.ds(1, bands - 1)], plane_send.at[order])
+            pack = packed and order == 0
             for way in range(2):
-                settle(relay.at[order, way], relay_send.at[way, order])
-                settle(recv.at[order, 1 + way, 1 - way], raw_send.at[way, order])
-                settle(recv.at[order, 1 + way, way], sum_send.at[way, order])
+                settle(lot(relay.at[order, way], way, pack), relay_send.at[way, order])
+                window = recv.at[order, 1 + way, 1 - way]
+                settle(lot(window, 1 - way, pack), raw_send.at[way, order])
+                settle(lot(recv.at[order, 1 + way, way], way, pack), sum_send.at[way, order])
         for copy in copies:
             copy.wait()
         total = got_e[0]
@@ -657,12 +696,12 @@
     tiles = -(-pairs // LANES)
     unit = cells // 2
     pitch = 8 * (-(-cells // 8) | 1)
-    slots = 4
+    slots = min(4, 2 * (tiles - 1))
     q_local, k_local = band_vectors.shape[0], band_vectors.shape[1]
     bands_n = band_vectors.shape[3]
     columns = 2 * qpoints.shape[1]
     halves = q_local // 4
-    rows = 4 * k_local
+    rows = 2 * k_local
     bands_own = bands_n // bands
     overlaps = sum(
         max(t * LANES, n * MODES) < min((t + 1) * LANES, (n + 1) * MODES)
@@ -690,10 +729,10 @@
             pltpu.VMEM((2 * k_local * kas, 2 * cells), bf16),
             pltpu.VMEM((columns * pitch, LANES), f32),
             pltpu.VMEM((slots, parts_count, unit, phonons, LANES), bf16),
-            pltpu.VMEM((tiles, kas, 2, halves, bands, rows, LANES), bf16),
-            pltpu.VMEM((tiles, 3, 2, halves, bands, rows, LANES), bf16),
-            pltpu.VMEM((tiles, 2, halves, bands, rows, LANES), bf16),
-            pltpu.VMEM((tiles, 2, halves, bands, rows, LANES), bf16),
+            pltpu.VMEM((tiles, kas, 2, halves, bands, 2, rows, LANES), bf16),
+            pltpu.VMEM((tiles, 3, 2, halves, bands, 2, rows, LANES), bf16),
+            pltpu.VMEM((tiles, 2, halves, bands, 2, rows, LANES), bf16),
+            pltpu.VMEM((tiles, 2, halves, bands, 2, rows, LANES), bf16),
             pltpu.VMEM((q_local, overlaps, LANES, 2 * LANES), bf16),
             pltpu.VMEM((q_local, bands_own, 2, bands * 2 * k_local, LANES), f32),
             pltpu.VMEM((2, bands_n, LANES), f32),

time: 43.7 us -> 43.5 us (level)
  no operation moved by 1% of the time
where the time goes in v5:
time: 43.5 us; the launch traced here: 43.3 us
  Pallas kernels  41.4 us (95%)
  other arithmetic  1.26 us (3%)
  between operations  0.64 us (1%)
    pallas_call x1, Pallas kernels, everything(): pl.pallas_call(functools.partial(ring_kernel, pairs), grid=(2,), in_specs...  41.4 us
    div x1, other arithmetic, on_device(): return (sums[0] / (q_total * NB), sums[1] / (k_total * NB))  1.26 us

profile of v5, /device:TPU:0, one launch (start us, length us, event | category | flops | bytes accessed | tf_op | source)
XLA Modules:
  0.0 43.3 jit_solution(1862307845168644137)
XLA Ops:
  0.6 41.4 %widths.1 = f32[2,4,120]{2,1,0:T(4,128)} custom-call(s32[3,16]{1,0:T(4,128)} %kpoints.1, s32[3,32]{1,0:T(4,128)} %qpoints.1, s32[3,320]{1,0:T(4,128)} %electron_cells.1, s32[3,320]{1,0:T(4,128)} %phonon_cells.1, bf16[4,2,120,120]{3,2,1,0:T(8,128)(2,1)} %modes.1, bf16[4,4,2,40,40]{4,3,2,1,0:T(8,128)(2,1)} %vectors.1, f32[4,4,40]{2,1,0:T(4,128)} %levels.1, ...), custom_call_target="tpu_custom_call" | custom-call | tf_op jit(solution)/shard_map/widths/pallas_call | solution.py:715
  42.0 1.3 %multiply_bitcast_fusion = (f32[4,120]{1,0:T(4,128)}, f32[4,120]{1,0:T(4,128)}) fusion(f32[2,4,120]{2,1,0:T(4,128)} %widths.1), kind=kLoop, calls=%fused_computation | loop fusion | flops 960 | bytes 7680 | tf_op jit(solution)/shard_map/div | solution.py:800

commit v6 on v5

--- a/solution.py
+++ b/solution.py
@@ -411,11 +411,31 @@
     def item(ref, way, to, pack):
         return ref.at[:, to, 0] if pack and way == 1 else ref.at[:, to]
 
+    def start(order, way, pack=False):
+        put(lot(parts.at[order, across, way], way, pack), lot(relay.at[order, way], way, pack),
+            relay_send.at[way, order], relay_recv.at[way, order], my_pb, (up, down)[way])
+
+    def contract_half(order, way):
+        for band in range(bands):
+            for inside in range(halves):
+                m = way * halves + inside
+                group = band * mine + m
+                right = jnp.concatenate(
+                    [
+                        jnp.concatenate([strip(q), strip(q_total + q)], axis=0)
+                        for q in (group * 2, group * 2 + 1)
+                    ],
+                    axis=1,
+                )
+                product = jnp.dot(wk[...], right, preferred_element_type=jnp.float32)
+                for ka in range(kas):
+                    block = product[ka * rows : (ka + 1) * rows]
+                    for member in range(2):
+                        parts[order, ka, way, inside, band, member] = block[
+                            :, member * LANES : (member + 1) * LANES
+                        ].astype(jnp.bfloat16)
+
     def send(order, pack=False):
-        for way, target in enumerate((up, down)):
-            put(lot(parts.at[order, across, way], way, pack), lot(relay.at[order, way], way, pack),
-                relay_send.at[way, order], relay_recv.at[way, order], my_pb, target)
-
         def raw(index, carry):
             to = lax.rem(my_pb + index, bands)
             for way, target in enumerate((down, up)):
@@ -541,6 +561,8 @@
     def _():
         contract(0, packed)
         pl.semaphore_wait(barrier, devices - 1)
+        start(0, 0, packed)
+        start(0, 1, packed)
         send(0, packed)
 
         def one_tile(tile, carry):
@@ -565,7 +587,9 @@
                     def _():
                         pass_on(tile - 1)
 
-            contract(tile + 1)
+            for way in range(2):
+                contract_half(tile + 1, way)
+                start(tile + 1, way)
             send(tile + 1)
 
 
@@ -575,8 +599,9 @@
         for order in range(tiles):
             recv[order, 0, :, :, my_pb] = parts[order, my_ka, :, :, my_pb]
         pass_on(tiles - 2, packed and tiles == 2)
+        pl.when(my_ka < kas - 1)(prepare)
         pass_on(tiles - 1)
-        prepare()
+        pl.when(my_ka == kas - 1)(prepare)
         started = set()
         for order in range(tiles):
             tile = tiles - 1 if order == 0 else order - 1

time: 43.5 us -> 43.4 us (level)
  no operation moved by 1% of the time
where the time goes in v6:
time: 43.4 us; the launch traced here: 43.2 us
  Pallas kernels  41.3 us (95%)
  other arithmetic  1.26 us (3%)
  between operations  0.64 us (1%)
    pallas_call x1, Pallas kernels, everything(): pl.pallas_call(functools.partial(ring_kernel, pairs), grid=(2,), in_specs...  41.3 us
    div x1, other arithmetic, on_device(): return (sums[0] / (q_total * NB), sums[1] / (k_total * NB))  1.26 us

profile of v6, /device:TPU:0, one launch (start us, length us, event | category | flops | bytes accessed | tf_op | source)
XLA Modules:
  0.0 43.2 jit_solution(10827198142240641387)
XLA Ops:
  0.6 41.3 %widths.1 = f32[2,4,120]{2,1,0:T(4,128)} custom-call(s32[3,16]{1,0:T(4,128)} %kpoints.1, s32[3,32]{1,0:T(4,128)} %qpoints.1, s32[3,320]{1,0:T(4,128)} %electron_cells.1, s32[3,320]{1,0:T(4,128)} %phonon_cells.1, bf16[4,2,120,120]{3,2,1,0:T(8,128)(2,1)} %modes.1, bf16[4,4,2,40,40]{4,3,2,1,0:T(8,128)(2,1)} %vectors.1, f32[4,4,40]{2,1,0:T(4,128)} %levels.1, ...), custom_call_target="tpu_custom_call" | custom-call | tf_op jit(solution)/shard_map/widths/pallas_call | solution.py:740
  41.9 1.3 %multiply_bitcast_fusion = (f32[4,120]{1,0:T(4,128)}, f32[4,120]{1,0:T(4,128)}) fusion(f32[2,4,120]{2,1,0:T(4,128)} %widths.1), kind=kLoop, calls=%fused_computation | loop fusion | flops 960 | bytes 7680 | tf_op jit(solution)/shard_map/div | solution.py:825
